TPU v7x, 32 devices: a whole 2x2x4 slice. The times are simulated.
32 devices in a mesh: gx: 4 (over y, x), gy: 4 (over z), gz: 2 (over core).
Axes of the slice: x: 2, y: 2, z: 4, core: 2. Of those that a mesh axis runs over, the one named last changes fastest.
Arguments:
- coarse: bfloat16 [2, 5, 8, 32, 128], P(None, None, 'gz', 'gx', 'gy'), may hold values from -1.5 to 1.5
- detail_x1: bfloat16 [2, 5, 8, 32, 128], P(None, None, 'gz', 'gx', 'gy'), may hold values from -1 to 1
- detail_y1: bfloat16 [2, 5, 8, 64, 128], P(None, None, 'gz', 'gx', 'gy'), may hold values from -1 to 1
- detail_x2: bfloat16 [2, 5, 8, 64, 256], P(None, None, 'gz', 'gx', 'gy'), may hold values from -1 to 1
- detail_y2: bfloat16 [2, 5, 8, 128, 256], P(None, None, 'gz', 'gx', 'gy'), may hold values from -1 to 1
- significance: int32 [2, 8, 16, 16], P(None, 'gz', 'gx', 'gy'), may hold values 0 or 1
- adjoint: float32 [5, 8, 128, 512], P(None, 'gz', 'gx', 'gy'), may hold values from -6 to 6
Outputs:
- adjoint_next: float32 [5, 8, 128, 512], P(None, 'gz', 'gx', 'gy')
Inputs may be any that keep to these rules, and one draw needn't show every extreme that they name: `significance`: each entry flags one tile.
All inputs are finite; a program needn't handle non-finite values. No bound on the sum of `significance` on one device may be relied on, other than what follows from the above.
Results may differ from a plain program's by a relative error of at most 0.0012.
Values may be sent and summed in bfloat16 or wider, within the bound.
A program may use at most 64 MiB of HBM per device.

v0:
```python
import jax
import jax.numpy as jnp
from jax import lax
from jax.sharding import PartitionSpec as P

time_step = 0.1
viscosity = 0.2
heat_ratio_less_one = 0.4


def with_halo(cells, sides, width, closed):
    for axis, dim in sides:
        count = lax.axis_size(axis)
        ends = count if closed else count - 1
        head = lax.slice_in_dim(cells, 0, width, axis=dim)
        tail = lax.slice_in_dim(cells, cells.shape[dim] - width, cells.shape[dim], axis=dim)
        cells = jnp.concatenate(
            [
                lax.ppermute(tail, axis, [(i, (i + 1) % count) for i in range(ends)]),
                cells,
                lax.ppermute(head, axis, [((i + 1) % count, i) for i in range(ends)]),
            ],
            axis=dim,
        )
    return cells


def alternate(padded, detail, axis_dim, length):
    centre = lax.slice_in_dim(padded, 2, length + 2, axis=axis_dim)
    behind = lax.slice_in_dim(padded, 1, length + 1, axis=axis_dim)
    ahead_one = lax.slice_in_dim(padded, 3, length + 3, axis=axis_dim)
    ahead_two = lax.slice_in_dim(padded, 4, length + 4, axis=axis_dim)
    odd_values = detail + (9.0 * (centre + ahead_one) - (behind + ahead_two)) / 16.0
    stacked = jnp.stack([centre, odd_values], axis=axis_dim + 1)
    target = list(centre.shape)
    target[axis_dim] = 2 * length
    return stacked.reshape(target)


def refine_x(coarse_part, detail):
    padded = with_halo(coarse_part.astype(jnp.bfloat16), (("gx", 3),), 2, True).astype(
        coarse_part.dtype
    )
    return alternate(padded, detail, 3, coarse_part.shape[3])


def refine_y(coarse_part, detail):
    padded = with_halo(coarse_part.astype(jnp.bfloat16), (("gy", 4),), 2, True).astype(
        coarse_part.dtype
    )
    return alternate(padded, detail, 4, coarse_part.shape[4])


def spread_mask(tile_flags, rows_tile, cols_tile):
    ones_block = jnp.ones((1, 1, 1, rows_tile, 1, cols_tile), jnp.float32)
    widened = tile_flags.astype(jnp.float32)[:, :, :, None, :, None] * ones_block
    return widened.reshape(
        tile_flags.shape[0],
        tile_flags.shape[1],
        tile_flags.shape[2] * rows_tile,
        tile_flags.shape[3] * cols_tile,
    )[:, None]


def face_flux(physical_variable_set, component):
    volumetric_matter = jnp.exp(0.5 * physical_variable_set[0])
    velocity = physical_variable_set[1:4]
    thermal_state_value = physical_variable_set[4]
    thermo_normal_stress = volumetric_matter * thermal_state_value
    normal_speed = velocity[component]
    velocity_norm_square = (
        velocity[0] * velocity[0] + velocity[1] * velocity[1] + velocity[2] * velocity[2]
    )
    whole_conserved_work = volumetric_matter * (
        thermal_state_value / heat_ratio_less_one + 0.5 * velocity_norm_square
    )
    mass_flux = volumetric_matter * normal_speed
    momenta = [mass_flux * velocity[which] for which in range(3)]
    momenta[component] = momenta[component] + thermo_normal_stress
    return jnp.stack(
        [mass_flux] + momenta + [normal_speed * (whole_conserved_work + thermo_normal_stress)]
    )


def face_term(upper_state, lower_state, upper_adjoint, lower_adjoint, component):
    middle_state = 0.5 * (upper_state + lower_state)
    jump = upper_adjoint - lower_adjoint
    unused, pullback = jax.vjp(lambda values: face_flux(values, component), middle_state)
    return pullback(jump)[0]


def adjoint_rims(adjoint_now):
    padded_xy = with_halo(adjoint_now.astype(jnp.bfloat16), (("gx", 2), ("gy", 3)), 1, True).astype(
        adjoint_now.dtype
    )
    padded_z = with_halo(adjoint_now.astype(jnp.bfloat16), (("gz", 1),), 1, False).astype(
        adjoint_now.dtype
    )
    return (padded_xy[:, :, :, 1:-1], padded_xy[:, :, 1:-1, :], padded_z)


def viscous_part(adjoint_now, extended, axis_dim, length):
    lower_adjoint = lax.slice_in_dim(extended, 0, length, axis=axis_dim)
    upper_adjoint = lax.slice_in_dim(extended, 2, length + 2, axis=axis_dim)
    return viscosity * (upper_adjoint + lower_adjoint - 2.0 * adjoint_now)


def rate_local(state_ext, adjoint_now, keep_bottom):
    adjoint_ext = adjoint_rims(adjoint_now)
    totals = jnp.zeros_like(adjoint_now)
    for component, axis_dim in ((0, 2), (1, 3), (2, 1)):
        length = adjoint_now.shape[axis_dim]
        extended = state_ext[component]
        adjoint_wide = adjoint_ext[component]
        face_terms = face_term(
            lax.slice_in_dim(extended, 1, length + 2, axis=axis_dim),
            lax.slice_in_dim(extended, 0, length + 1, axis=axis_dim),
            lax.slice_in_dim(adjoint_wide, 1, length + 2, axis=axis_dim),
            lax.slice_in_dim(adjoint_wide, 0, length + 1, axis=axis_dim),
            component,
        )
        first_face = lax.slice_in_dim(face_terms, 0, 1, axis=axis_dim)
        if component == 2:
            first_face = first_face * keep_bottom
        lower_terms = jnp.concatenate(
            [first_face, lax.slice_in_dim(face_terms, 1, length, axis=axis_dim)], axis=axis_dim
        )
        totals = (
            totals
            + 0.5 * lax.slice_in_dim(face_terms, 1, length + 1, axis=axis_dim)
            + 0.5 * lower_terms
        )
        totals = totals + viscous_part(adjoint_now, adjoint_wide, axis_dim, length)
    return totals


def shards(coarse, detail_x1, detail_y1, detail_x2, detail_y2, significance, adjoint):
    refined = refine_x(coarse.astype(jnp.float32), detail_x1.astype(jnp.float32))
    refined = refine_y(refined, detail_y1.astype(jnp.float32))
    refined = refine_x(refined, detail_x2.astype(jnp.float32) * spread_mask(significance, 4, 16))
    primitives = refine_y(refined, detail_y2.astype(jnp.float32) * spread_mask(significance, 8, 16))
    state_xy = None
    keep_bottom = jnp.where(lax.axis_index("gz") > 0, 1.0, 0.0).astype(jnp.float32)
    state_xy = with_halo(primitives.astype(jnp.bfloat16), (("gx", 3), ("gy", 4)), 1, True).astype(
        primitives.dtype
    )
    state_z = with_halo(primitives.astype(jnp.bfloat16), (("gz", 2),), 1, False).astype(
        primitives.dtype
    )
    first_ext = (state_xy[0][:, :, :, 1:-1], state_xy[0][:, :, 1:-1, :], state_z[0])
    second_ext = (state_xy[1][:, :, :, 1:-1], state_xy[1][:, :, 1:-1, :], state_z[1])
    first_rate = rate_local(first_ext, adjoint, keep_bottom)
    middle = adjoint + time_step * first_rate
    second_rate = rate_local(second_ext, middle, keep_bottom)
    return adjoint + 0.5 * time_step * (first_rate + second_rate)


def solution(mesh):
    return jax.shard_map(
        shards,
        mesh=mesh,
        in_specs=(
            P(None, None, "gz", "gx", "gy"),
            P(None, None, "gz", "gx", "gy"),
            P(None, None, "gz", "gx", "gy"),
            P(None, None, "gz", "gx", "gy"),
            P(None, None, "gz", "gx", "gy"),
            P(None, "gz", "gx", "gy"),
            P(None, "gz", "gx", "gy"),
        ),
        out_specs=P(None, "gz", "gx", "gy"),
        check_vma=False,
    )
```

profile of v0, /device:TPU:0, one launch (start us, length us, event | category | flops | bytes accessed | tf_op | source)
XLA Modules:
  0.0 116.3 jit_solution(7990939088714170230)
XLA Ops:
  0.0 1.1 fusion.115
  1.1 3.0 %collective-permute-start = (bf16[2,5,4,2,32]{4,3,2,1,0:T(2,128)(2,1)S(1)}, bf16[2,5,4,2,32]{4,3,2,1,0:T(2,128)(2,1)S(1)}, u32[]{:S(2)}, u32[]{:S(2)}) collective-permute-start(bf16[2,5,4,2,32]{4,3,2,1,0:T(2,128)(2,1)S(1)} %get-tuple-element.101), channel_id=1, source_target_pairs={{0,8},{8,16},{16,24},{24,0},{1,9},{9,17},{17,25},{25,1},{2,10},{10... | collective-permute-start | bytes 15368 | tf_op jit(solution)/shard_map/ppermute | solution.py:19
  4.1 1.0 collective-permute-start.1
  5.1 1.0 convert_element_type.87
  6.1 1.0 collective-permute-start.12
  7.2 1.9 %collective-permute-start.13 = (bf16[5,4,1,128]{3,1,2,0:T(4,128)(2,1)S(1)}, bf16[5,4,1,128]{3,1,2,0:T(4,128)(2,1)S(1)}, u32[]{:S(2)}, u32[]{:S(2)}) collective-permute-start(bf16[5,4,1,128]{3,1,2,0:T(4,128)(2,1)S(1)} %copy.143), channel_id=1, source_target_pairs={{8,0},{16,8},{24,16},{0,24},{9,1},{17,9},{25,17},{1,25},{10,2},{18... | collective-permute-start | bytes 15368 | tf_op jit(solution)/shard_map/ppermute | solution.py:21
  9.1 0.6 fusion.114
  9.8 1.3 %collective-permute-start.18 = (bf16[5,1,32,128]{3,2,1,0:T(8,128)(2,1)}, bf16[5,1,32,128]{3,2,1,0:T(8,128)(2,1)S(1)}, u32[]{:S(2)}, u32[]{:S(2)}) collective-permute-start(bf16[5,1,32,128]{3,2,1,0:T(8,128)(2,1)} %get-tuple-element.99), channel_id=1, source_target_pairs={{0,1},{2,3},{4,5},{6,7},{8,9},{10,11},{12,13},{14,15},{16,17},{18,... | collective-permute-start | bytes 122888 | tf_op jit(solution)/shard_map/ppermute | solution.py:19
  11.1 0.7 convert_element_type.81
  12.5 1.3 %collective-permute-start.19 = (bf16[5,1,32,128]{3,2,1,0:T(8,128)(2,1)}, bf16[5,1,32,128]{3,2,1,0:T(8,128)(2,1)S(1)}, u32[]{:S(2)}, u32[]{:S(2)}) collective-permute-start(bf16[5,1,32,128]{3,2,1,0:T(8,128)(2,1)} %get-tuple-element.100), channel_id=1, source_target_pairs={{1,0},{3,2},{5,4},{7,6},{9,8},{11,10},{13,12},{15,14},{17,16},{19,... | collective-permute-start | bytes 122888 | tf_op jit(solution)/shard_map/ppermute | solution.py:21
  14.4 2.0 %collective-permute-start.2 = (bf16[2,5,4,16,2]{4,3,2,1,0:T(8,128)(2,1)S(1)}, bf16[2,5,4,16,2]{4,3,2,1,0:T(8,128)(2,1)S(1)}, u32[]{:S(2)}, u32[]{:S(2)}) collective-permute-start(bf16[2,5,4,16,2]{4,3,2,1,0:T(8,128)(2,1)S(1)} %get-tuple-element.97), channel_id=1, source_target_pairs={{0,2},{2,4},{4,6},{6,0},{1,3},{3,5},{5,7},{7,1},{8,10},{10,12},{12... | collective-permute-start | bytes 7688 | tf_op jit(solution)/shard_map/ppermute | solution.py:19
  16.5 2.1 %collective-permute-start.3 = (bf16[2,5,4,16,2]{4,3,2,1,0:T(8,128)(2,1)S(1)}, bf16[2,5,4,16,2]{4,3,2,1,0:T(8,128)(2,1)S(1)}, u32[]{:S(2)}, u32[]{:S(2)}) collective-permute-start(bf16[2,5,4,16,2]{4,3,2,1,0:T(8,128)(2,1)S(1)} %get-tuple-element.98), channel_id=1, source_target_pairs={{2,0},{4,2},{6,4},{0,6},{3,1},{5,3},{7,5},{1,7},{10,8},{12,10},{14... | collective-permute-start | bytes 7688 | tf_op jit(solution)/shard_map/ppermute | solution.py:21
  18.9 4.4 %collective-permute-done.2 = bf16[2,5,4,16,2]{4,3,2,1,0:T(8,128)(2,1)S(1)} collective-permute-done((bf16[2,5,4,16,2]{4,3,2,1,0:T(8,128)(2,1)S(1)}, bf16[2,5,4,16,2]{4,3,2,1,0:T(8,128)(2,1)S(1)}, u32[]{:S(2)}, u32[]{:S(2)}) %collective-permute-start.2) | collective-permute-done | bytes 2592 | tf_op jit(solution)/shard_map/ppermute | solution.py:19
  23.3 2.2 %collective-permute-start.15 = (bf16[5,4,34,1]{3,2,1,0:T(8,128)(2,1)S(1)}, bf16[5,4,34,1]{3,2,1,0:T(8,128)(2,1)S(1)}, u32[]{:S(2)}, u32[]{:S(2)}) collective-permute-start(bf16[5,4,34,1]{3,2,1,0:T(8,128)(2,1)S(1)} %get-tuple-element.90), channel_id=1, source_target_pairs={{2,0},{4,2},{6,4},{0,6},{3,1},{5,3},{7,5},{1,7},{10,8},{12,10},{14... | collective-permute-start | bytes 4088 | tf_op jit(solution)/shard_map/ppermute | solution.py:21
  25.6 1.8 %collective-permute-done.3 = bf16[2,5,4,16,2]{4,3,2,1,0:T(8,128)(2,1)S(1)} collective-permute-done((bf16[2,5,4,16,2]{4,3,2,1,0:T(8,128)(2,1)S(1)}, bf16[2,5,4,16,2]{4,3,2,1,0:T(8,128)(2,1)S(1)}, u32[]{:S(2)}, u32[]{:S(2)}) %collective-permute-start.3) | collective-permute-done | bytes 2592 | tf_op jit(solution)/shard_map/ppermute | solution.py:21
  27.6 0.4 fusion.68
  28.1 0.5 copy.129
  28.6 0.3 fusion.104
  28.9 0.3 copy.130
  29.3 0.3 copy.131
  29.6 1.7 %collective-permute-done.14 = bf16[5,4,34,1]{3,2,1,0:T(8,128)(2,1)S(1)} collective-permute-done((bf16[5,4,34,1]{3,2,1,0:T(8,128)(2,1)S(1)}, bf16[5,4,34,1]{3,2,1,0:T(8,128)(2,1)S(1)}, u32[]{:S(2)}, u32[]{:S(2)}) %collective-permute-start.14) | collective-permute-done | bytes 1392 | tf_op jit(solution)/shard_map/ppermute | solution.py:19
  31.3 1.3 %collective-permute-start.5 = (bf16[2,5,4,2,64]{4,2,3,1,0:T(4,128)(2,1)S(1)}, bf16[2,5,4,2,64]{4,2,3,1,0:T(4,128)(2,1)S(1)}, u32[]{:S(2)}, u32[]{:S(2)}) collective-permute-start(bf16[2,5,4,2,64]{4,2,3,1,0:T(4,128)(2,1)S(1)} %copy.131), channel_id=1, source_target_pairs={{8,0},{16,8},{24,16},{0,24},{9,1},{17,9},{25,17},{1,25},{10,2},{18... | collective-permute-start | bytes 30728 | tf_op jit(solution)/shard_map/ppermute | solution.py:21
  32.6 3.1 %collective-permute-done.15 = bf16[5,4,34,1]{3,2,1,0:T(8,128)(2,1)S(1)} collective-permute-done((bf16[5,4,34,1]{3,2,1,0:T(8,128)(2,1)S(1)}, bf16[5,4,34,1]{3,2,1,0:T(8,128)(2,1)S(1)}, u32[]{:S(2)}, u32[]{:S(2)}) %collective-permute-start.15) | collective-permute-done | bytes 1392 | tf_op jit(solution)/shard_map/ppermute | solution.py:21
  35.7 0.3 maximum_convert_fusion.2
  37.1 0.3 copy.135
  37.6 0.5 collective-permute-start.6
  38.1 3.3 %collective-permute-start.7 = (bf16[2,5,4,32,2]{4,3,2,1,0:T(8,128)(2,1)S(1)}, bf16[2,5,4,32,2]{4,3,2,1,0:T(8,128)(2,1)S(1)}, u32[]{:S(2)}, u32[]{:S(2)}) collective-permute-start(bf16[2,5,4,32,2]{4,3,2,1,0:T(8,128)(2,1)S(1)} %get-tuple-element.86), channel_id=1, source_target_pairs={{2,0},{4,2},{6,4},{0,6},{3,1},{5,3},{7,5},{1,7},{10,8},{12,10},{14... | collective-permute-start | bytes 15368 | tf_op jit(solution)/shard_map/ppermute | solution.py:21
  41.5 1.1 slice_subtract_fusion.1
  42.6 7.4 %collective-permute-done.6 = bf16[2,5,4,32,2]{4,3,2,1,0:T(8,128)(2,1)S(1)} collective-permute-done((bf16[2,5,4,32,2]{4,3,2,1,0:T(8,128)(2,1)S(1)}, bf16[2,5,4,32,2]{4,3,2,1,0:T(8,128)(2,1)S(1)}, u32[]{:S(2)}, u32[]{:S(2)}) %collective-permute-start.6) | collective-permute-done | bytes 5152 | tf_op jit(solution)/shard_map/ppermute | solution.py:19
  50.0 4.6 %collective-permute-done.7 = bf16[2,5,4,32,2]{4,3,2,1,0:T(8,128)(2,1)S(1)} collective-permute-done((bf16[2,5,4,32,2]{4,3,2,1,0:T(8,128)(2,1)S(1)}, bf16[2,5,4,32,2]{4,3,2,1,0:T(8,128)(2,1)S(1)}, u32[]{:S(2)}, u32[]{:S(2)}) %collective-permute-start.7) | collective-permute-done | bytes 5152 | tf_op jit(solution)/shard_map/ppermute | solution.py:21
  54.6 0.3 maximum_convert_fusion.4
  55.1 0.7 fusion.56
  56.0 0.9 copy.136
  56.9 1.7 %fusion.103 = (bf16[2,5,4,1,128]{3,4,2,1,0:T(8,128)(2,1)}, bf16[2,5,4,1,128]{3,4,2,1,0:T(8,128)(2,1)S(1)}) fusion(bf16[2,5,4,32,128]{3,4,2,1,0:T(8,128)(2,1)S(1)} %bitcast.28), kind=kLoop, calls=%fused_computation.276 | loop fusion | bytes 40960 | tf_op jit(solution)/shard_map/slice | solution.py:16
  58.6 1.8 %copy.137 = bf16[2,5,4,1,128]{4,2,3,1,0:T(4,128)(2,1)S(1)} copy(bf16[2,5,4,1,128]{3,4,2,1,0:T(8,128)(2,1)} %get-tuple-element.39) | data formatting | bytes 20480 | tf_op jit(solution)/shard_map/slice | solution.py:16
  60.4 1.0 collective-permute-start.8
  61.4 0.5 copy.138
  61.9 1.9 %collective-permute-start.9 = (bf16[2,5,4,1,128]{4,2,3,1,0:T(4,128)(2,1)S(1)}, bf16[2,5,4,1,128]{4,2,3,1,0:T(4,128)(2,1)S(1)}, u32[]{:S(2)}, u32[]{:S(2)}) collective-permute-start(bf16[2,5,4,1,128]{4,2,3,1,0:T(4,128)(2,1)S(1)} %copy.138), channel_id=1, source_target_pairs={{8,0},{16,8},{24,16},{0,24},{9,1},{17,9},{25,17},{1,25},{10,2},{18... | collective-permute-start | bytes 30728 | tf_op jit(solution)/shard_map/ppermute | solution.py:21
  64.1 0.6 copy.140
  64.7 0.4 collective-permute-done.8
  65.1 0.7 copy.139
  66.2 1.2 %collective-permute-start.10 = (bf16[2,5,4,34,1]{4,3,2,1,0:T(8,128)(2,1)S(1)}, bf16[2,5,4,34,1]{4,3,2,1,0:T(8,128)(2,1)S(1)}, u32[]{:S(2)}, u32[]{:S(2)}) collective-permute-start(bf16[2,5,4,34,1]{4,3,2,1,0:T(8,128)(2,1)S(1)} %get-tuple-element.81), channel_id=1, source_target_pairs={{0,2},{2,4},{4,6},{6,0},{1,3},{3,5},{5,7},{7,1},{8,10},{10,12},{12... | collective-permute-start | bytes 8168 | tf_op jit(solution)/shard_map/ppermute | solution.py:19
  67.5 2.7 %collective-permute-start.11 = (bf16[2,5,4,34,1]{4,3,2,1,0:T(8,128)(2,1)S(1)}, bf16[2,5,4,34,1]{4,3,2,1,0:T(8,128)(2,1)S(1)}, u32[]{:S(2)}, u32[]{:S(2)}) collective-permute-start(bf16[2,5,4,34,1]{4,3,2,1,0:T(8,128)(2,1)S(1)} %get-tuple-element.82), channel_id=1, source_target_pairs={{2,0},{4,2},{6,4},{0,6},{3,1},{5,3},{7,5},{1,7},{10,8},{12,10},{14... | collective-permute-start | bytes 8168 | tf_op jit(solution)/shard_map/ppermute | solution.py:21
  70.1 1.3 %collective-permute-start.16 = (bf16[2,5,1,32,128]{4,3,2,1,0:T(8,128)(2,1)S(1)}, bf16[2,5,1,32,128]{4,3,2,1,0:T(8,128)(2,1)S(1)}, u32[]{:S(2)}, u32[]{:S(2)}) collective-permute-start(bf16[2,5,1,32,128]{4,3,2,1,0:T(8,128)(2,1)S(1)} %get-tuple-element.83), channel_id=1, source_target_pairs={{0,1},{2,3},{4,5},{6,7},{8,9},{10,11},{12,13},{14,15},{16,17},{18,... | collective-permute-start | bytes 245768 | tf_op jit(solution)/shard_map/ppermute | solution.py:19
  71.4 9.1 %collective-permute-done.10 = bf16[2,5,4,34,1]{4,3,2,1,0:T(8,128)(2,1)S(1)} collective-permute-done((bf16[2,5,4,34,1]{4,3,2,1,0:T(8,128)(2,1)S(1)}, bf16[2,5,4,34,1]{4,3,2,1,0:T(8,128)(2,1)S(1)}, u32[]{:S(2)}, u32[]{:S(2)}) %collective-permute-start.10) | collective-permute-done | bytes 2752 | tf_op jit(solution)/shard_map/ppermute | solution.py:19
  80.5 1.5 %collective-permute-start.17 = (bf16[2,5,1,32,128]{4,3,2,1,0:T(8,128)(2,1)S(1)}, bf16[2,5,1,32,128]{4,3,2,1,0:T(8,128)(2,1)S(1)}, u32[]{:S(2)}, u32[]{:S(2)}) collective-permute-start(bf16[2,5,1,32,128]{4,3,2,1,0:T(8,128)(2,1)S(1)} %get-tuple-element.84), channel_id=1, source_target_pairs={{1,0},{3,2},{5,4},{7,6},{9,8},{11,10},{13,12},{15,14},{17,16},{19,... | collective-permute-start | bytes 245768 | tf_op jit(solution)/shard_map/ppermute | solution.py:21
  82.0 4.3 %collective-permute-done.11 = bf16[2,5,4,34,1]{4,3,2,1,0:T(8,128)(2,1)S(1)} collective-permute-done((bf16[2,5,4,34,1]{4,3,2,1,0:T(8,128)(2,1)S(1)}, bf16[2,5,4,34,1]{4,3,2,1,0:T(8,128)(2,1)S(1)}, u32[]{:S(2)}, u32[]{:S(2)}) %collective-permute-start.11) | collective-permute-done | bytes 2752 | tf_op jit(solution)/shard_map/ppermute | solution.py:21
  86.3 0.7 maximum_convert_fusion
  87.8 0.7 copy-done
  88.7 0.3 fusion.8
  89.7 0.8 copy-done.2
  91.1 0.7 copy-done.3
  91.9 0.7 fusion.55
  92.6 2.4 %collective-permute-start.20 = (bf16[5,4,1,128]{3,1,2,0:T(4,128)(2,1)S(1)}, bf16[5,4,1,128]{3,1,2,0:T(4,128)(2,1)S(1)}, u32[]{:S(2)}, u32[]{:S(2)}) collective-permute-start(bf16[5,4,1,128]{3,1,2,0:T(4,128)(2,1)S(1)} %copy.149), channel_id=1, source_target_pairs={{0,8},{8,16},{16,24},{24,0},{1,9},{9,17},{17,25},{25,1},{2,10},{10... | collective-permute-start | bytes 15368 | tf_op jit(solution)/shard_map/ppermute | solution.py:19
  95.0 0.6 collective-permute-start.21
  95.6 1.3 %collective-permute-start.24 = (bf16[5,1,32,128]{3,2,1,0:T(8,128)(2,1)S(1)}, bf16[5,1,32,128]{3,2,1,0:T(8,128)(2,1)S(1)}, u32[]{:S(2)}, u32[]{:S(2)}) collective-permute-start(bf16[5,1,32,128]{3,2,1,0:T(8,128)(2,1)S(1)} %get-tuple-element.93), channel_id=1, source_target_pairs={{0,1},{2,3},{4,5},{6,7},{8,9},{10,11},{12,13},{14,15},{16,17},{18,... | collective-permute-start | bytes 122888 | tf_op jit(solution)/shard_map/ppermute | solution.py:19
  96.9 1.3 %collective-permute-start.25 = (bf16[5,1,32,128]{3,2,1,0:T(8,128)(2,1)S(1)}, bf16[5,1,32,128]{3,2,1,0:T(8,128)(2,1)S(1)}, u32[]{:S(2)}, u32[]{:S(2)}) collective-permute-start(bf16[5,1,32,128]{3,2,1,0:T(8,128)(2,1)S(1)} %get-tuple-element.94), channel_id=1, source_target_pairs={{1,0},{3,2},{5,4},{7,6},{9,8},{11,10},{13,12},{15,14},{17,16},{19,... | collective-permute-start | bytes 122888 | tf_op jit(solution)/shard_map/ppermute | solution.py:21
  98.2 0.4 collective-permute-done.21
  98.8 0.6 collective-permute-start.22
  99.4 3.3 %collective-permute-start.23 = (bf16[5,4,34,1]{3,2,1,0:T(8,128)(2,1)S(1)}, bf16[5,4,34,1]{3,2,1,0:T(8,128)(2,1)S(1)}, u32[]{:S(2)}, u32[]{:S(2)}) collective-permute-start(bf16[5,4,34,1]{3,2,1,0:T(8,128)(2,1)S(1)} %get-tuple-element.88), channel_id=1, source_target_pairs={{2,0},{4,2},{6,4},{0,6},{3,1},{5,3},{7,5},{1,7},{10,8},{12,10},{14... | collective-permute-start | bytes 4088 | tf_op jit(solution)/shard_map/ppermute | solution.py:21
  102.7 5.9 %collective-permute-done.22 = bf16[5,4,34,1]{3,2,1,0:T(8,128)(2,1)S(1)} collective-permute-done((bf16[5,4,34,1]{3,2,1,0:T(8,128)(2,1)S(1)}, bf16[5,4,34,1]{3,2,1,0:T(8,128)(2,1)S(1)}, u32[]{:S(2)}, u32[]{:S(2)}) %collective-permute-start.22) | collective-permute-done | bytes 1392 | tf_op jit(solution)/shard_map/ppermute | solution.py:19
  108.7 4.1 %collective-permute-done.23 = bf16[5,4,34,1]{3,2,1,0:T(8,128)(2,1)S(1)} collective-permute-done((bf16[5,4,34,1]{3,2,1,0:T(8,128)(2,1)S(1)}, bf16[5,4,34,1]{3,2,1,0:T(8,128)(2,1)S(1)}, u32[]{:S(2)}, u32[]{:S(2)}) %collective-permute-start.23) | collective-permute-done | bytes 1392 | tf_op jit(solution)/shard_map/ppermute | solution.py:21
  112.8 0.3 maximum_convert_fusion.3
  114.9 1.3 %fusion.19 = f32[5,4,32,128]{3,2,1,0:T(8,128)} fusion(f32[5,4,32,128]{3,2,1,0:T(8,128)S(1)} %copy-done.3, f32[5,4,32,128]{3,2,1,0:T(8,128)S(1)} %get-tuple-element.18, f32[5,6,32,128]{3,2,1,0:T(8,128)S(1)} %maximum_convert_fusion.6, f32[5,5,32,128]{3,2,1,0:T(8,128)S(1)} %pad_add_fusion.2, f32[5,4,34,130]{3,2,1,0:T(8,128)S(1)} %maximum_convert_fusion.3, ...), kind=kLoop, calls=%fused_computation.69 | loop fusion | flops 2375680 | bytes 4915200 | tf_op jit(solution)/shard_map/add | solution.py:155
  (121 shorter events, 8.3 us)
Async XLA Ops:
  0.0 13.8 %copy-start.5 = (bf16[2,5,4,8,32]{4,3,2,1,0:T(8,128)(2,1)S(1)}, bf16[2,5,4,8,32]{4,3,2,1,0:T(8,128)(2,1)}, u32[]{:S(2)}) copy-start(bf16[2,5,4,8,32]{4,3,2,1,0:T(8,128)(2,1)} %param.7) | copy-start | bytes 61444
  1.1 11.4 %collective-permute-start = (bf16[2,5,4,2,32]{4,3,2,1,0:T(2,128)(2,1)S(1)}, bf16[2,5,4,2,32]{4,3,2,1,0:T(2,128)(2,1)S(1)}, u32[]{:S(2)}, u32[]{:S(2)}) collective-permute-start(bf16[2,5,4,2,32]{4,3,2,1,0:T(2,128)(2,1)S(1)} %get-tuple-element.101), channel_id=1, source_target_pairs={{0,8},{8,16},{16,24},{24,0},{1,9},{9,17},{17,25},{25,1},{2,10},{10... | collective-permute-start | bytes 15368 | tf_op jit(solution)/shard_map/ppermute | solution.py:19
  4.1 9.9 %copy-start.8 = (bf16[2,5,4,8,32]{4,3,2,1,0:T(8,128)(2,1)S(1)}, bf16[2,5,4,8,32]{4,3,2,1,0:T(8,128)(2,1)}, u32[]{:S(2)}) copy-start(bf16[2,5,4,8,32]{4,3,2,1,0:T(8,128)(2,1)} %param.8) | copy-start | bytes 61444
  4.1 9.7 %collective-permute-start.1 = (bf16[2,5,4,2,32]{4,3,2,1,0:T(2,128)(2,1)S(1)}, bf16[2,5,4,2,32]{4,3,2,1,0:T(2,128)(2,1)S(1)}, u32[]{:S(2)}, u32[]{:S(2)}) collective-permute-start(bf16[2,5,4,2,32]{4,3,2,1,0:T(2,128)(2,1)S(1)} %get-tuple-element.102), channel_id=1, source_target_pairs={{8,0},{16,8},{24,16},{0,24},{9,1},{17,9},{25,17},{1,25},{10,2},{18... | collective-permute-start | bytes 15368 | tf_op jit(solution)/shard_map/ppermute | solution.py:21
  6.1 29.6 %copy-start.1 = (bf16[5,4,32,128]{3,2,1,0:T(8,128)(2,1)}, bf16[5,4,32,128]{3,2,1,0:T(8,128)(2,1)S(1)}, u32[]{:S(2)}) copy-start(bf16[5,4,32,128]{3,2,1,0:T(8,128)(2,1)S(1)} %convert_element_type.87) | copy-start | bytes 491524
  6.1 10.3 %collective-permute-start.12 = (bf16[5,4,1,128]{3,1,2,0:T(4,128)(2,1)S(1)}, bf16[5,4,1,128]{3,1,2,0:T(4,128)(2,1)S(1)}, u32[]{:S(2)}, u32[]{:S(2)}) collective-permute-start(bf16[5,4,1,128]{3,1,2,0:T(4,128)(2,1)S(1)} %copy.142), channel_id=1, source_target_pairs={{0,8},{8,16},{16,24},{24,0},{1,9},{9,17},{17,25},{25,1},{2,10},{10... | collective-permute-start | bytes 15368 | tf_op jit(solution)/shard_map/ppermute | solution.py:19
  7.2 11.4 %collective-permute-start.13 = (bf16[5,4,1,128]{3,1,2,0:T(4,128)(2,1)S(1)}, bf16[5,4,1,128]{3,1,2,0:T(4,128)(2,1)S(1)}, u32[]{:S(2)}, u32[]{:S(2)}) collective-permute-start(bf16[5,4,1,128]{3,1,2,0:T(4,128)(2,1)S(1)} %copy.143), channel_id=1, source_target_pairs={{8,0},{16,8},{24,16},{0,24},{9,1},{17,9},{25,17},{1,25},{10,2},{18... | collective-permute-start | bytes 15368 | tf_op jit(solution)/shard_map/ppermute | solution.py:21
  9.8 79.9 %collective-permute-start.18 = (bf16[5,1,32,128]{3,2,1,0:T(8,128)(2,1)}, bf16[5,1,32,128]{3,2,1,0:T(8,128)(2,1)S(1)}, u32[]{:S(2)}, u32[]{:S(2)}) collective-permute-start(bf16[5,1,32,128]{3,2,1,0:T(8,128)(2,1)} %get-tuple-element.99), channel_id=1, source_target_pairs={{0,1},{2,3},{4,5},{6,7},{8,9},{10,11},{12,13},{14,15},{16,17},{18,... | collective-permute-start | bytes 122888 | tf_op jit(solution)/shard_map/ppermute | solution.py:19
  12.5 77.2 %collective-permute-start.19 = (bf16[5,1,32,128]{3,2,1,0:T(8,128)(2,1)}, bf16[5,1,32,128]{3,2,1,0:T(8,128)(2,1)S(1)}, u32[]{:S(2)}, u32[]{:S(2)}) collective-permute-start(bf16[5,1,32,128]{3,2,1,0:T(8,128)(2,1)} %get-tuple-element.100), channel_id=1, source_target_pairs={{1,0},{3,2},{5,4},{7,6},{9,8},{11,10},{13,12},{15,14},{17,16},{19,... | collective-permute-start | bytes 122888 | tf_op jit(solution)/shard_map/ppermute | solution.py:21
  14.1 13.5 %copy-start.6 = (bf16[2,5,4,16,32]{4,3,2,1,0:T(8,128)(2,1)S(1)}, bf16[2,5,4,16,32]{4,3,2,1,0:T(8,128)(2,1)}, u32[]{:S(2)}) copy-start(bf16[2,5,4,16,32]{4,3,2,1,0:T(8,128)(2,1)} %param.9) | copy-start | bytes 122884
  14.4 8.9 %collective-permute-start.2 = (bf16[2,5,4,16,2]{4,3,2,1,0:T(8,128)(2,1)S(1)}, bf16[2,5,4,16,2]{4,3,2,1,0:T(8,128)(2,1)S(1)}, u32[]{:S(2)}, u32[]{:S(2)}) collective-permute-start(bf16[2,5,4,16,2]{4,3,2,1,0:T(8,128)(2,1)S(1)} %get-tuple-element.97), channel_id=1, source_target_pairs={{0,2},{2,4},{4,6},{6,0},{1,3},{3,5},{5,7},{7,1},{8,10},{10,12},{12... | collective-permute-start | bytes 7688 | tf_op jit(solution)/shard_map/ppermute | solution.py:19
  16.5 10.9 %collective-permute-start.3 = (bf16[2,5,4,16,2]{4,3,2,1,0:T(8,128)(2,1)S(1)}, bf16[2,5,4,16,2]{4,3,2,1,0:T(8,128)(2,1)S(1)}, u32[]{:S(2)}, u32[]{:S(2)}) collective-permute-start(bf16[2,5,4,16,2]{4,3,2,1,0:T(8,128)(2,1)S(1)} %get-tuple-element.98), channel_id=1, source_target_pairs={{2,0},{4,2},{6,4},{0,6},{3,1},{5,3},{7,5},{1,7},{10,8},{12,10},{14... | collective-permute-start | bytes 7688 | tf_op jit(solution)/shard_map/ppermute | solution.py:21
  18.8 12.5 %collective-permute-start.14 = (bf16[5,4,34,1]{3,2,1,0:T(8,128)(2,1)S(1)}, bf16[5,4,34,1]{3,2,1,0:T(8,128)(2,1)S(1)}, u32[]{:S(2)}, u32[]{:S(2)}) collective-permute-start(bf16[5,4,34,1]{3,2,1,0:T(8,128)(2,1)S(1)} %get-tuple-element.89), channel_id=1, source_target_pairs={{0,2},{2,4},{4,6},{6,0},{1,3},{3,5},{5,7},{7,1},{8,10},{10,12},{12... | collective-permute-start | bytes 4088 | tf_op jit(solution)/shard_map/ppermute | solution.py:19
  23.3 12.4 %collective-permute-start.15 = (bf16[5,4,34,1]{3,2,1,0:T(8,128)(2,1)S(1)}, bf16[5,4,34,1]{3,2,1,0:T(8,128)(2,1)S(1)}, u32[]{:S(2)}, u32[]{:S(2)}) collective-permute-start(bf16[5,4,34,1]{3,2,1,0:T(8,128)(2,1)S(1)} %get-tuple-element.90), channel_id=1, source_target_pairs={{2,0},{4,2},{6,4},{0,6},{3,1},{5,3},{7,5},{1,7},{10,8},{12,10},{14... | collective-permute-start | bytes 4088 | tf_op jit(solution)/shard_map/ppermute | solution.py:21
  29.3 7.1 %collective-permute-start.4 = (bf16[2,5,4,2,64]{4,2,3,1,0:T(4,128)(2,1)S(1)}, bf16[2,5,4,2,64]{4,2,3,1,0:T(4,128)(2,1)S(1)}, u32[]{:S(2)}, u32[]{:S(2)}) collective-permute-start(bf16[2,5,4,2,64]{4,2,3,1,0:T(4,128)(2,1)S(1)} %copy.130), channel_id=1, source_target_pairs={{0,8},{8,16},{16,24},{24,0},{1,9},{9,17},{17,25},{25,1},{2,10},{10... | collective-permute-start | bytes 30728 | tf_op jit(solution)/shard_map/ppermute | solution.py:19
  29.6 7.0 %copy-start.7 = (bf16[2,5,4,16,64]{4,3,2,1,0:T(8,128)(2,1)S(1)}, bf16[2,5,4,16,64]{4,3,2,1,0:T(8,128)(2,1)}, u32[]{:S(2)}) copy-start(bf16[2,5,4,16,64]{4,3,2,1,0:T(8,128)(2,1)} %param.10) | copy-start | bytes 245764
  31.3 5.1 %collective-permute-start.5 = (bf16[2,5,4,2,64]{4,2,3,1,0:T(4,128)(2,1)S(1)}, bf16[2,5,4,2,64]{4,2,3,1,0:T(4,128)(2,1)S(1)}, u32[]{:S(2)}, u32[]{:S(2)}) collective-permute-start(bf16[2,5,4,2,64]{4,2,3,1,0:T(4,128)(2,1)S(1)} %copy.131), channel_id=1, source_target_pairs={{8,0},{16,8},{24,16},{0,24},{9,1},{17,9},{25,17},{1,25},{10,2},{18... | collective-permute-start | bytes 30728 | tf_op jit(solution)/shard_map/ppermute | solution.py:21
  37.6 12.4 %collective-permute-start.6 = (bf16[2,5,4,32,2]{4,3,2,1,0:T(8,128)(2,1)S(1)}, bf16[2,5,4,32,2]{4,3,2,1,0:T(8,128)(2,1)S(1)}, u32[]{:S(2)}, u32[]{:S(2)}) collective-permute-start(bf16[2,5,4,32,2]{4,3,2,1,0:T(8,128)(2,1)S(1)} %get-tuple-element.85), channel_id=1, source_target_pairs={{0,2},{2,4},{4,6},{6,0},{1,3},{3,5},{5,7},{7,1},{8,10},{10,12},{12... | collective-permute-start | bytes 15368 | tf_op jit(solution)/shard_map/ppermute | solution.py:19
  38.1 16.5 %collective-permute-start.7 = (bf16[2,5,4,32,2]{4,3,2,1,0:T(8,128)(2,1)S(1)}, bf16[2,5,4,32,2]{4,3,2,1,0:T(8,128)(2,1)S(1)}, u32[]{:S(2)}, u32[]{:S(2)}) collective-permute-start(bf16[2,5,4,32,2]{4,3,2,1,0:T(8,128)(2,1)S(1)} %get-tuple-element.86), channel_id=1, source_target_pairs={{2,0},{4,2},{6,4},{0,6},{3,1},{5,3},{7,5},{1,7},{10,8},{12,10},{14... | collective-permute-start | bytes 15368 | tf_op jit(solution)/shard_map/ppermute | solution.py:21
  42.6 12.5 %copy-start.4 = (bf16[2,5,4,32,64]{4,3,2,1,0:T(8,128)(2,1)S(1)}, bf16[2,5,4,32,64]{4,3,2,1,0:T(8,128)(2,1)}, u32[]{:S(2)}) copy-start(bf16[2,5,4,32,64]{4,3,2,1,0:T(8,128)(2,1)} %param.11) | copy-start | bytes 491524
  60.4 4.7 %collective-permute-start.8 = (bf16[2,5,4,1,128]{4,2,3,1,0:T(4,128)(2,1)S(1)}, bf16[2,5,4,1,128]{4,2,3,1,0:T(4,128)(2,1)}, u32[]{:S(2)}, u32[]{:S(2)}) collective-permute-start(bf16[2,5,4,1,128]{4,2,3,1,0:T(4,128)(2,1)S(1)} %copy.137), channel_id=1, source_target_pairs={{0,8},{8,16},{16,24},{24,0},{1,9},{9,17},{17,25},{25,1},{2,10},{10... | collective-permute-start | bytes 30728 | tf_op jit(solution)/shard_map/ppermute | solution.py:19
  61.9 3.9 %collective-permute-start.9 = (bf16[2,5,4,1,128]{4,2,3,1,0:T(4,128)(2,1)S(1)}, bf16[2,5,4,1,128]{4,2,3,1,0:T(4,128)(2,1)S(1)}, u32[]{:S(2)}, u32[]{:S(2)}) collective-permute-start(bf16[2,5,4,1,128]{4,2,3,1,0:T(4,128)(2,1)S(1)} %copy.138), channel_id=1, source_target_pairs={{8,0},{16,8},{24,16},{0,24},{9,1},{17,9},{25,17},{1,25},{10,2},{18... | collective-permute-start | bytes 30728 | tf_op jit(solution)/shard_map/ppermute | solution.py:21
  66.2 14.3 %collective-permute-start.10 = (bf16[2,5,4,34,1]{4,3,2,1,0:T(8,128)(2,1)S(1)}, bf16[2,5,4,34,1]{4,3,2,1,0:T(8,128)(2,1)S(1)}, u32[]{:S(2)}, u32[]{:S(2)}) collective-permute-start(bf16[2,5,4,34,1]{4,3,2,1,0:T(8,128)(2,1)S(1)} %get-tuple-element.81), channel_id=1, source_target_pairs={{0,2},{2,4},{4,6},{6,0},{1,3},{3,5},{5,7},{7,1},{8,10},{10,12},{12... | collective-permute-start | bytes 8168 | tf_op jit(solution)/shard_map/ppermute | solution.py:19
  67.5 18.8 %collective-permute-start.11 = (bf16[2,5,4,34,1]{4,3,2,1,0:T(8,128)(2,1)S(1)}, bf16[2,5,4,34,1]{4,3,2,1,0:T(8,128)(2,1)S(1)}, u32[]{:S(2)}, u32[]{:S(2)}) collective-permute-start(bf16[2,5,4,34,1]{4,3,2,1,0:T(8,128)(2,1)S(1)} %get-tuple-element.82), channel_id=1, source_target_pairs={{2,0},{4,2},{6,4},{0,6},{3,1},{5,3},{7,5},{1,7},{10,8},{12,10},{14... | collective-permute-start | bytes 8168 | tf_op jit(solution)/shard_map/ppermute | solution.py:21
  70.1 20.4 %collective-permute-start.16 = (bf16[2,5,1,32,128]{4,3,2,1,0:T(8,128)(2,1)S(1)}, bf16[2,5,1,32,128]{4,3,2,1,0:T(8,128)(2,1)S(1)}, u32[]{:S(2)}, u32[]{:S(2)}) collective-permute-start(bf16[2,5,1,32,128]{4,3,2,1,0:T(8,128)(2,1)S(1)} %get-tuple-element.83), channel_id=1, source_target_pairs={{0,1},{2,3},{4,5},{6,7},{8,9},{10,11},{12,13},{14,15},{16,17},{18,... | collective-permute-start | bytes 245768 | tf_op jit(solution)/shard_map/ppermute | solution.py:19
  80.5 10.0 %collective-permute-start.17 = (bf16[2,5,1,32,128]{4,3,2,1,0:T(8,128)(2,1)S(1)}, bf16[2,5,1,32,128]{4,3,2,1,0:T(8,128)(2,1)S(1)}, u32[]{:S(2)}, u32[]{:S(2)}) collective-permute-start(bf16[2,5,1,32,128]{4,3,2,1,0:T(8,128)(2,1)S(1)} %get-tuple-element.84), channel_id=1, source_target_pairs={{1,0},{3,2},{5,4},{7,6},{9,8},{11,10},{13,12},{15,14},{17,16},{19,... | collective-permute-start | bytes 245768 | tf_op jit(solution)/shard_map/ppermute | solution.py:21
  87.4 1.1 copy-start
  89.5 0.9 copy-start.2
  90.9 1.0 copy-start.3
  92.6 5.6 %collective-permute-start.20 = (bf16[5,4,1,128]{3,1,2,0:T(4,128)(2,1)S(1)}, bf16[5,4,1,128]{3,1,2,0:T(4,128)(2,1)S(1)}, u32[]{:S(2)}, u32[]{:S(2)}) collective-permute-start(bf16[5,4,1,128]{3,1,2,0:T(4,128)(2,1)S(1)} %copy.149), channel_id=1, source_target_pairs={{0,8},{8,16},{16,24},{24,0},{1,9},{9,17},{17,25},{25,1},{2,10},{10... | collective-permute-start | bytes 15368 | tf_op jit(solution)/shard_map/ppermute | solution.py:19
  95.0 3.6 %collective-permute-start.21 = (bf16[5,4,1,128]{3,1,2,0:T(4,128)(2,1)S(1)}, bf16[5,4,1,128]{3,1,2,0:T(4,128)(2,1)S(1)}, u32[]{:S(2)}, u32[]{:S(2)}) collective-permute-start(bf16[5,4,1,128]{3,1,2,0:T(4,128)(2,1)S(1)} %copy.150), channel_id=1, source_target_pairs={{8,0},{16,8},{24,16},{0,24},{9,1},{17,9},{25,17},{1,25},{10,2},{18... | collective-permute-start | bytes 15368 | tf_op jit(solution)/shard_map/ppermute | solution.py:21
  95.6 18.9 %collective-permute-start.24 = (bf16[5,1,32,128]{3,2,1,0:T(8,128)(2,1)S(1)}, bf16[5,1,32,128]{3,2,1,0:T(8,128)(2,1)S(1)}, u32[]{:S(2)}, u32[]{:S(2)}) collective-permute-start(bf16[5,1,32,128]{3,2,1,0:T(8,128)(2,1)S(1)} %get-tuple-element.93), channel_id=1, source_target_pairs={{0,1},{2,3},{4,5},{6,7},{8,9},{10,11},{12,13},{14,15},{16,17},{18,... | collective-permute-start | bytes 122888 | tf_op jit(solution)/shard_map/ppermute | solution.py:19
  96.9 17.6 %collective-permute-start.25 = (bf16[5,1,32,128]{3,2,1,0:T(8,128)(2,1)S(1)}, bf16[5,1,32,128]{3,2,1,0:T(8,128)(2,1)S(1)}, u32[]{:S(2)}, u32[]{:S(2)}) collective-permute-start(bf16[5,1,32,128]{3,2,1,0:T(8,128)(2,1)S(1)} %get-tuple-element.94), channel_id=1, source_target_pairs={{1,0},{3,2},{5,4},{7,6},{9,8},{11,10},{13,12},{15,14},{17,16},{19,... | collective-permute-start | bytes 122888 | tf_op jit(solution)/shard_map/ppermute | solution.py:21
  98.8 9.8 %collective-permute-start.22 = (bf16[5,4,34,1]{3,2,1,0:T(8,128)(2,1)S(1)}, bf16[5,4,34,1]{3,2,1,0:T(8,128)(2,1)S(1)}, u32[]{:S(2)}, u32[]{:S(2)}) collective-permute-start(bf16[5,4,34,1]{3,2,1,0:T(8,128)(2,1)S(1)} %get-tuple-element.87), channel_id=1, source_target_pairs={{0,2},{2,4},{4,6},{6,0},{1,3},{3,5},{5,7},{7,1},{8,10},{10,12},{12... | collective-permute-start | bytes 4088 | tf_op jit(solution)/shard_map/ppermute | solution.py:19
  99.4 13.4 %collective-permute-start.23 = (bf16[5,4,34,1]{3,2,1,0:T(8,128)(2,1)S(1)}, bf16[5,4,34,1]{3,2,1,0:T(8,128)(2,1)S(1)}, u32[]{:S(2)}, u32[]{:S(2)}) collective-permute-start(bf16[5,4,34,1]{3,2,1,0:T(8,128)(2,1)S(1)} %get-tuple-element.88), channel_id=1, source_target_pairs={{2,0},{4,2},{6,4},{0,6},{3,1},{5,3},{7,5},{1,7},{10,8},{12,10},{14... | collective-permute-start | bytes 4088 | tf_op jit(solution)/shard_map/ppermute | solution.py:21
where the time goes:
time: 117 us; the launch traced here: 116 us
  waiting for transfers between devices  47.2 us (40%)
  starting transfers between devices  40.3 us (34%)
  local copies, waits for them, and re-layouts  14.4 us (12%)
  other arithmetic  13.4 us (11%)
    ppermute x13, waiting for transfers between devices, with_halo(): lax.ppermute(tail, axis, [(i, (i + 1) % count) for i in range(ends)])  28.9 us
    ppermute x13, starting transfers between devices, with_halo(): lax.ppermute(head, axis, [((i + 1) % count, i) for i in range(ends)])  24.4 us
    ppermute x13, waiting for transfers between devices, with_halo(): lax.ppermute(head, axis, [((i + 1) % count, i) for i in range(ends)])  18.3 us
    ppermute x13, starting transfers between devices, with_halo(): lax.ppermute(tail, axis, [(i, (i + 1) % count) for i in range(ends)])  15.8 us
    slice x17, local copies, waits for them, and re-layouts, with_halo(): lax.slice_in_dim(cells, cells.shape[dim] - width, cells.shape[dim], axis=...  6.58 us
  transfers between devices with their start and end apart: 26, of which 12 were waited for; matrix products, arithmetic and copies ran while one was open for 19% of the time, Pallas kernels for 0%

commit v1 on v0

v1 whole, which is shorter than its diff:
```python
import functools

import jax
import jax.numpy as jnp
import ml_dtypes
import numpy as np
from jax import lax
from jax.experimental import pallas as pl
from jax.experimental.pallas import tpu as pltpu
from jax.sharding import PartitionSpec as P

time_step = 0.1
viscosity = 0.2
heat_ratio_less_one = 0.4
f32 = jnp.float32
bf16 = jnp.bfloat16
MESH = pl.DeviceIdType.MESH
segments = ((0, 320, 32), (320, 640, 32), (640, 1280, 32), (1280, 1920, 64), (1920, 3200, 64))


def predict(index):
    k = index // 2
    if index % 2 == 0:
        return {("c", k): 1.0}
    return {
        ("d", k): 1.0,
        ("c", k): 9 / 16,
        ("c", k + 1): 9 / 16,
        ("c", k - 1): -1 / 16,
        ("c", k + 2): -1 / 16,
    }


def predict_twice(index):
    whole = {}
    for (kind, k), weight in predict(index).items():
        if kind == "d":
            whole[("e", k)] = weight
            continue
        whole[("m", k)] = weight
        for key, inner in predict(k).items():
            whole[key] = whole.get(key, 0.0) + weight * inner
    return whole


def lane_of(k, length):
    if k < 0:
        return 69 + k
    return k if k < length else 64 + k - length


def y_matrices():
    mats = np.zeros((4, 128, 256), np.float32)
    columns = [(y, y) for y in range(128)] + [(128, 128), (-1, 255)]
    for y, column in columns:
        for (kind, k), weight in predict_twice(y).items():
            which = "cdme".index(kind)
            mats[which, lane_of(k, 32 if which < 2 else 64), column] += weight
    return mats.astype(ml_dtypes.bfloat16)


def x_matrix():
    mat = np.zeros((48, 64), np.float32)
    for x in range(-1, 33):
        row = x + 8
        for (kind, k), weight in predict_twice(x).items():
            if kind == "c":
                at = 50 + k if k < 0 else (k if k < 8 else 56 + k - 8)
            elif kind == "d":
                at = 50 if k < 0 else (8 + k if k < 8 else 59)
            elif kind == "m":
                at = 53 + k if k < 0 else (16 + k if k < 16 else 60 + k - 16)
            else:
                at = 53 if k < 0 else 32 + k
            mat[row, at] += weight
    mat[7, 54] = 1.0
    mat[40, 62] = 1.0
    return np.concatenate([mat, mat], axis=1).astype(ml_dtypes.bfloat16)


def pick_matrices():
    pick = np.zeros((2, 16, 64), np.float32)
    for which, width in ((0, 32), (1, 64)):
        for j in range(3):
            pick[which, j, j] = 1.0
        pick[which, 11, width - 2] = 1.0
        pick[which, 12, width - 1] = 1.0
    return pick.astype(ml_dtypes.bfloat16)


def place_matrix():
    place = np.zeros((8, 128), np.float32)
    for j in range(5):
        place[j, 64 + j] = 1.0
    return place


def face(mean, jump, k):
    q, u, t = mean[0], mean[1:4], mean[4]
    rho = jnp.exp(0.5 * q)
    speed = u[k]
    half_square = 0.5 * (u[0] * u[0] + u[1] * u[1] + u[2] * u[2])
    enthalpy = (1.0 / heat_ratio_less_one + 1.0) * t + half_square
    inner = jump[0] + jump[1] * u[0] + jump[2] * u[1] + jump[3] * u[2] + jump[4] * enthalpy
    flow = rho * speed
    grads = [flow * (jump[1 + j] + jump[4] * u[j]) for j in range(3)]
    grads[k] = grads[k] + rho * inner
    dq = 0.5 * (flow * inner + rho * t * jump[1 + k])
    dt = rho * jump[1 + k] + (1.0 / heat_ratio_less_one + 1.0) * flow * jump[4]
    return [dq] + grads + [dt]


def kernel(
    c_ref, x1_ref, y1_ref, x2_ref, y2_ref, sig_ref, adj_ref, ay_ref, ax_ref, pick_ref, place_ref,
    out_ref,
    tiles, mask_x, mask_y, ext, send_first, send_last, recv_first, recv_last,
    rows_low, rows_high, recv_low, recv_high,
    mapped, mapped_y2, state, edge, state_z,
    adj_ext, adj_edge, mid_ext, mid_edge,
    ax_send, ax_recv, ay_send, ay_recv, az_send, az_recv, gx_terms, gz_terms,
    send_sem, recv_sem,
):
    gx, gy, gz = lax.axis_index("gx"), lax.axis_index("gy"), lax.axis_index("gz")
    nx, ny = lax.axis_size("gx"), lax.axis_size("gy")
    x_up, x_down = {"gx": lax.rem(gx + 1, nx)}, {"gx": lax.rem(gx + nx - 1, nx)}
    y_up, y_down = {"gy": lax.rem(gy + 1, ny)}, {"gy": lax.rem(gy + ny - 1, ny)}
    z_other = {"gz": 1 - gz}
    barrier = pltpu.get_barrier_semaphore()
    for peer in (x_up, x_down, y_up, y_down, z_other):
        pl.semaphore_signal(barrier, inc=1, device_id=peer, device_id_type=MESH)

    def remote(index, source, target, peer):
        return pltpu.make_async_remote_copy(
            src_ref=source,
            dst_ref=target,
            send_sem=send_sem.at[index],
            recv_sem=recv_sem.at[index],
            device_id=peer,
            device_id_type=MESH,
        )

    lane = lax.broadcasted_iota(jnp.int32, (8, 128), 1)
    lane_wide = lax.broadcasted_iota(jnp.int32, (32, 128), 1)

    lane_tile = lax.broadcasted_iota(jnp.int32, (4, 64), 1) // 16
    row_half = lax.broadcasted_iota(jnp.int32, (8, 64), 0) < 4
    for c in range(2):
        for z in range(4):
            flags = sig_ref[c, z].astype(f32)
            wide = jnp.zeros((4, 64), f32)
            for t in range(4):
                wide = jnp.where(lane_tile == t, flags[:, t : t + 1], wide)
            tiles[c, z, 0:4] = wide
            each = [jnp.broadcast_to(tiles[c, z, t : t + 1], (8, 64)) for t in range(4)]
            for t in range(4):
                mask_y[c, z, 8 * t : 8 * t + 8] = each[t]
            for t in range(2):
                mask_x[c, z, 8 * t : 8 * t + 8] = jnp.where(row_half, each[2 * t], each[2 * t + 1])

    kept_x2 = x2_ref[...].astype(f32).reshape(2, 5, 4, 16, 64) * mask_x[...][:, None]
    kept_y2 = y2_ref[...].astype(f32).reshape(2, 5, 4, 32, 64) * mask_y[...][:, None]
    values = (
        c_ref[...],
        x1_ref[...],
        y1_ref[...],
        kept_x2.reshape(640, 64).astype(bf16),
        kept_y2.reshape(1280, 64).astype(bf16),
    )
    for (begin, end, width), value in zip(segments, values):
        pick = pick_ref[0 if width == 32 else 1][:, 0:width]
        ends = lax.dot_general(pick, value, (((1,), (1,)), ((), ())), preferred_element_type=f32)
        send_first[:, begin:end] = ends[0:8].astype(bf16)
        send_last[:, begin:end] = ends[8:16].astype(bf16)

    def pack_rims(source, which):
        for i in range(20):
            v, z = i // 4, i % 4
            ax_send[which, 0, i : i + 1] = source[v, z + 1, 8:9]
            ax_send[which, 1, i : i + 1] = source[v, z + 1, 39:40]
        first = jnp.zeros((32, 128), f32)
        last = jnp.zeros((32, 128), f32)
        for i in range(20):
            plane = source[i // 4, i % 4 + 1, 8:40]
            first = jnp.where(lane_wide == i, plane[:, 0:1], first)
            last = jnp.where(lane_wide == i, plane[:, 127:128], last)
        ay_send[which, 0] = first
        ay_send[which, 1] = last

    def rim_copies(source, which):
        base = 5 + 5 * which
        return [
            remote(base, ax_send.at[which, 0], ax_recv.at[which, 1], x_down),
            remote(base + 1, ax_send.at[which, 1], ax_recv.at[which, 0], x_up),
            remote(base + 2, ay_send.at[which, 0], ay_recv.at[which, 1], y_down),
            remote(base + 3, ay_send.at[which, 1], ay_recv.at[which, 0], y_up),
            remote(base + 4, source, az_recv.at[which], z_other),
        ]

    z_side = 3 - 3 * gz
    pl.semaphore_wait(barrier, 5)
    y_copies = [
        remote(0, send_first, recv_first, y_down),
        remote(1, send_last, recv_last, y_up),
    ]
    for copy in y_copies:
        copy.start()

    adj_ext[...] = jnp.zeros_like(adj_ext)
    for i in range(20):
        adj_ext[i // 4, i % 4 + 1, 8:40] = adj_ref[i // 4, i % 4]
    pack_rims(adj_ext, 0)
    adj_copies = rim_copies(adj_ref.at[:, z_side], 0)
    for copy in adj_copies:
        copy.start()

    ext[...] = jnp.zeros_like(ext)
    for (begin, end, width), value in zip(segments, values):
        ext[begin:end, 0:width] = value.astype(f32)
    mid_ext[...] = jnp.zeros_like(mid_ext)

    def fill_rims(target, target_edge, which):
        for i in range(20):
            v, z = i // 4, i % 4
            target[v, z + 1, 7:8] = ax_recv[which, 0, i : i + 1]
            target[v, z + 1, 40:41] = ax_recv[which, 1, i : i + 1]
            target_edge[v, z] = jnp.where(
                lane_wide == 0, ay_recv[which, 1, :, i : i + 1], ay_recv[which, 0, :, i : i + 1]
            )
        for v in range(5):
            plane = az_recv[which, v]
            target[v, 0, 8:40] = jnp.where(gz > 0, plane, 0.0)
            target[v, 5, 8:40] = jnp.where(gz > 0, 0.0, plane)

    for copy in y_copies:
        copy.wait()
    joined = recv_first[...].astype(f32) + recv_last[...].astype(f32)
    ext[...] += jnp.dot(joined.T, place_ref[...], preferred_element_type=f32)

    coarse_e = ext[0:320].reshape(40, 8, 128)
    x1_e = ext[320:640].reshape(40, 8, 128)
    y1_e = ext[640:1280].reshape(40, 16, 128)
    x2_e = ext[1280:1920].reshape(40, 16, 128)
    y2_e = ext[1920:3200].reshape(40, 32, 128)
    blank = jnp.zeros((40, 1, 128), f32)
    low = jnp.concatenate(
        [coarse_e[:, 6:8], x1_e[:, 7:8], y1_e[:, 14:16], x2_e[:, 15:16], y2_e[:, 31:32], blank], 1
    )
    high = jnp.concatenate(
        [coarse_e[:, 0:3], x1_e[:, 0:1], y1_e[:, 0:2], y2_e[:, 0:1], blank], 1
    )
    rows_low[...] = low.reshape(320, 128).astype(bf16)
    rows_high[...] = high.reshape(320, 128).astype(bf16)
    x_copies = [
        remote(2, rows_low, recv_low, x_up),
        remote(3, rows_high, recv_high, x_down),
    ]
    for copy in x_copies:
        copy.start()

    for (begin, end, width), which, at in zip(segments, (0, 0, 1, 2, 3), (0, 8, 16, 32, None)):
        product = jnp.dot(
            ext[begin:end].astype(bf16), ay_ref[which], preferred_element_type=f32
        ).reshape(40, (end - begin) // 40, 256)
        if at is None:
            mapped_y2[...] = product
        else:
            mapped[:, at : at + (end - begin) // 40] = product

    for copy in adj_copies:
        copy.wait()
    fill_rims(adj_ext, adj_edge, 0)

    row_kind = lax.broadcasted_iota(jnp.int32, (320, 128), 0) % 8
    for copy in x_copies:
        copy.wait()
    for buffer, at, bounds in (
        (recv_low, 48, ((0, 3), (3, 5), (5, 6), (6, 8))),
        (recv_high, 56, ((0, 4), (4, 6), (6, 6), (6, 8))),
    ):
        received = buffer[...].astype(f32)
        total = jnp.zeros((320, 256), f32)
        for which, (begin, end) in enumerate(bounds):
            if begin < end:
                part = jnp.where((row_kind >= begin) & (row_kind < end), received, 0.0)
                total = total + jnp.dot(
                    part.astype(bf16), ay_ref[which], preferred_element_type=f32
                )
        mapped[:, at : at + 8] = total.reshape(40, 8, 256)

    def synthesize(cv, carry):
        for z in range(4):
            p = cv * 4 + z
            exact = mapped[p]
            coarse_bits = exact.astype(bf16)
            rest = (exact - coarse_bits.astype(f32)).astype(bf16)
            whole = jnp.dot(
                ax_ref[...],
                jnp.concatenate([coarse_bits, rest], axis=0),
                preferred_element_type=f32,
            )
            extra = mapped_y2[p]
            state[cv, z + 1, 0:8] = whole[0:8, 0:128]
            state[cv, z + 1, 8:40] = whole[8:40, 0:128] + extra[:, 0:128]
            state[cv, z + 1, 40:48] = whole[40:48, 0:128]
            edge[cv, z] = whole[8:40, 128:256] + extra[:, 128:256]
        return carry

    lax.fori_loop(0, 10, synthesize, 0)
    state_copy = remote(4, state.at[:, z_side + 1, 8:40], state_z, z_other)
    state_copy.start()
    state_copy.wait()
    for cv in range(10):
        plane = state_z[cv]
        state[cv, 0, 8:40] = jnp.where(gz > 0, plane, 0.0)
        state[cv, 5, 8:40] = jnp.where(gz > 0, 0.0, plane)

    keep_bottom = jnp.where(gz > 0, 1.0, 0.0).astype(f32)

    def rate(base, source, source_edge, finish):
        def z_faces(k, carry):
            for r in range(4):
                at = slice(8 + 8 * r, 16 + 8 * r)
                mean = [0.5 * (state[base + v, k, at] + state[base + v, k + 1, at]) for v in range(5)]
                jump = [source[v, k + 1, at] - source[v, k, at] for v in range(5)]
                terms = face(mean, jump, 2)
                factor = jnp.where(k == 0, keep_bottom, 1.0)
                for v in range(5):
                    gz_terms[v, k, 8 * r : 8 * r + 8] = terms[v] * factor
            return carry

        lax.fori_loop(0, 5, z_faces, 0)

        def plane(z, carry):
            for r in range(5):
                low_at, high_at = slice(7 + 8 * r, 15 + 8 * r), slice(8 + 8 * r, 16 + 8 * r)
                mean = [
                    0.5 * (state[base + v, z + 1, low_at] + state[base + v, z + 1, high_at])
                    for v in range(5)
                ]
                jump = [source[v, z + 1, high_at] - source[v, z + 1, low_at] for v in range(5)]
                terms = face(mean, jump, 0)
                for v in range(5):
                    gx_terms[v, 8 * r : 8 * r + 8] = terms[v]
            for r in range(4):
                at, rows = slice(8 + 8 * r, 16 + 8 * r), slice(8 * r, 8 * r + 8)
                here = [state[base + v, z + 1, at] for v in range(5)]
                rim = [edge[base + v, z, rows] for v in range(5)]
                adj = [source[v, z + 1, at] for v in range(5)]
                adj_rim = [source_edge[v, z, rows] for v in range(5)]

                def ahead(a, b):
                    return pltpu.roll(jnp.where(lane == 0, b, a), 127, 1)

                def behind(a, b):
                    return pltpu.roll(jnp.where(lane == 127, b, a), 1, 1)

                adj_up = [ahead(adj[v], adj_rim[v]) for v in range(5)]
                adj_down = [behind(adj[v], adj_rim[v]) for v in range(5)]
                up = face(
                    [0.5 * (here[v] + ahead(here[v], rim[v])) for v in range(5)],
                    [adj_up[v] - adj[v] for v in range(5)],
                    1,
                )
                down = face(
                    [0.5 * (here[v] + behind(here[v], rim[v])) for v in range(5)],
                    [adj[v] - adj_down[v] for v in range(5)],
                    1,
                )
                for v in range(5):
                    halves = (
                        up[v]
                        + down[v]
                        + gx_terms[v, rows]
                        + gx_terms[v, 8 * r + 1 : 8 * r + 9]
                        + gz_terms[v, z, rows]
                        + gz_terms[v, z + 1, rows]
                    )
                    around = (
                        adj_up[v]
                        + adj_down[v]
                        + source[v, z + 1, 7 + 8 * r : 15 + 8 * r]
                        + source[v, z + 1, 9 + 8 * r : 17 + 8 * r]
                        + source[v, z, at]
                        + source[v, z + 2, at]
                    )
                    finish(v, z, rows, at, 0.5 * halves + viscosity * (around - 6.0 * adj[v]))
            return carry

        lax.fori_loop(0, 4, plane, 0)

    def finish_first(v, z, rows, at, value):
        held = adj_ext[v, z + 1, at]
        mid_ext[v, z + 1, at] = held + time_step * value
        out_ref[v, z, rows] = held + 0.5 * time_step * value

    def finish_second(v, z, rows, at, value):
        out_ref[v, z, rows] += 0.5 * time_step * value

    rate(0, adj_ext, adj_edge, finish_first)
    pack_rims(mid_ext, 1)
    mid_copies = rim_copies(mid_ext.at[:, z_side + 1, 8:40], 1)
    for copy in mid_copies:
        copy.start()
    for copy in mid_copies:
        copy.wait()
    fill_rims(mid_ext, mid_edge, 1)
    rate(5, mid_ext, mid_edge, finish_second)


def shards(coarse, detail_x1, detail_y1, detail_x2, detail_y2, significance, adjoint):
    vmem = pl.BlockSpec(memory_space=pltpu.VMEM)
    return pl.pallas_call(
        kernel,
        out_shape=jax.ShapeDtypeStruct(adjoint.shape, f32),
        in_specs=[vmem] * 11,
        out_specs=vmem,
        scratch_shapes=[
            pltpu.VMEM((2, 4, 8, 64), f32),
            pltpu.VMEM((2, 4, 16, 64), f32),
            pltpu.VMEM((2, 4, 32, 64), f32),
            pltpu.VMEM((3200, 128), f32),
            pltpu.VMEM((8, 3200), bf16),
            pltpu.VMEM((8, 3200), bf16),
            pltpu.VMEM((8, 3200), bf16),
            pltpu.VMEM((8, 3200), bf16),
            pltpu.VMEM((320, 128), bf16),
            pltpu.VMEM((320, 128), bf16),
            pltpu.VMEM((320, 128), bf16),
            pltpu.VMEM((320, 128), bf16),
            pltpu.VMEM((40, 64, 256), f32),
            pltpu.VMEM((40, 32, 256), f32),
            pltpu.VMEM((10, 6, 48, 128), f32),
            pltpu.VMEM((10, 4, 32, 128), f32),
            pltpu.VMEM((10, 32, 128), f32),
            pltpu.VMEM((5, 6, 48, 128), f32),
            pltpu.VMEM((5, 4, 32, 128), f32),
            pltpu.VMEM((5, 6, 48, 128), f32),
            pltpu.VMEM((5, 4, 32, 128), f32),
            pltpu.VMEM((2, 2, 24, 128), f32),
            pltpu.VMEM((2, 2, 24, 128), f32),
            pltpu.VMEM((2, 2, 32, 128), f32),
            pltpu.VMEM((2, 2, 32, 128), f32),
            pltpu.VMEM((8, 128), f32),
            pltpu.VMEM((2, 5, 32, 128), f32),
            pltpu.VMEM((5, 40, 128), f32),
            pltpu.VMEM((5, 5, 32, 128), f32),
            pltpu.SemaphoreType.DMA((15,)),
            pltpu.SemaphoreType.DMA((15,)),
        ],
        compiler_params=pltpu.CompilerParams(collective_id=0, has_side_effects=True),
    )(
        coarse.reshape(320, 32),
        detail_x1.reshape(320, 32),
        detail_y1.reshape(640, 32),
        detail_x2.reshape(640, 64),
        detail_y2.reshape(1280, 64),
        significance,
        adjoint,
        jnp.asarray(y_matrices()),
        jnp.asarray(x_matrix()),
        jnp.asarray(pick_matrices()),
        jnp.asarray(place_matrix()),
    )


def solution(mesh):
    return jax.shard_map(
        shards,
        mesh=mesh,
        in_specs=(
            P(None, None, "gz", "gx", "gy"),
            P(None, None, "gz", "gx", "gy"),
            P(None, None, "gz", "gx", "gy"),
            P(None, None, "gz", "gx", "gy"),
            P(None, None, "gz", "gx", "gy"),
            P(None, "gz", "gx", "gy"),
            P(None, "gz", "gx", "gy"),
        ),
        out_specs=P(None, "gz", "gx", "gy"),
        check_vma=False,
    )
```

time: 117 us -> 29.5 us (0.25)
  waiting for transfers between devices: 47.2 us -> 0 us
  starting transfers between devices: 40.3 us -> 0 us
  Pallas kernels: 0 us -> 27.6 us
  other arithmetic: 13.4 us -> 0 us
  local copies, waits for them, and re-layouts: 14.4 us -> 1.72 us
    ppermute x26 -> x0, waiting for transfers between devices: 47.2 us -> none  [the longest x13 28.9 us: with_halo(): lax.ppermute(tail, axis, [(i, (i + 1) % count) for i in range(ends)])]
    ppermute x26 -> x0, starting transfers between devices: 40.3 us -> none  [the longest x13 24.4 us: with_halo(): lax.ppermute(head, axis, [((i + 1) % count, i) for i in range(ends)])]
    pallas_call x0 -> x1, Pallas kernels: none -> 27.6 us  [shards(): pl.pallas_call(kernel, out_shape=jax.ShapeDtypeStruct(adjoint.shape, f32)...]
    slice x23 -> x0, local copies, waits for them, and re-layouts: 7.42 us -> none  [the longest x17 6.58 us: with_halo(): lax.slice_in_dim(cells, cells.shape[dim] - width, cells.shape[dim], axis=...]
    convert_element_type x13 -> x0, other arithmetic: 4.61 us -> none  [the longest x2 1.65 us: adjoint_rims(): adjoint_now.astype(jnp.bfloat16)]
    another operation x8 -> x0, local copies, waits for them, and re-layouts: 2.26 us -> none  [alternate(): stacked = jnp.stack([centre, odd_values], axis=axis_dim + 1)]
    sub x6 -> x0, other arithmetic: 1.98 us -> none  [face_term(): jump = upper_adjoint - lower_adjoint]
    another operation x8 -> x0, other arithmetic: 1.98 us -> none  [alternate(): stacked = jnp.stack([centre, odd_values], axis=axis_dim + 1)]
  transfers between devices with their start and end apart: 26 -> 0, of which waited for: 12 -> 0; matrix products, arithmetic and copies ran while one was open for 19% -> 0% of each run, Pallas kernels for 0% -> 0%
where the time goes in v1:
time: 29.5 us; the launch traced here: 29.3 us
  Pallas kernels  27.6 us (94%)
  local copies, waits for them, and re-layouts  1.72 us (6%)
    pallas_call x1, Pallas kernels, shards(): pl.pallas_call(kernel, out_shape=jax.ShapeDtypeStruct(adjoint.shape, f32)...  27.6 us
    unnamed x1, local copies, waits for them, and re-layouts  1.72 us

profile of v1, /device:TPU:0, one launch (start us, length us, event | category | flops | bytes accessed | tf_op | source)
XLA Modules:
  0.0 29.3 jit_solution(9310987893896810094)
XLA Ops:
  0.0 27.6 %shard_map.109 = f32[5,4,32,128]{3,2,1,0:T(8,128)} custom-call(bf16[320,32]{1,0:T(8,128)(2,1)} %bitcast.8, bf16[320,32]{1,0:T(8,128)(2,1)} %bitcast.9, bf16[640,32]{1,0:T(8,128)(2,1)} %bitcast.6, bf16[640,64]{1,0:T(8,128)(2,1)} %bitcast.7, bf16[1280,64]{1,0:T(8,128)(2,1)} %bitcast.5, s32[2,4,4,4]{3,2,1,0:T(4,128)} %sig_ref.1, f32[5,4,32,128]{3,2,1,0:T(8,128)} %adj_ref.1, ...), custom_call_target="tpu_custom_call" | custom-call | tf_op jit(solution)/shard_map/pallas_call | solution.py:412
  27.6 1.7 %copy.13 = f32[5,4,32,128]{3,2,1,0:T(8,128)} copy(f32[5,4,32,128]{3,2,1,0:T(8,128)} %shard_map.109) | data formatting | bytes 655360

commit v2 on v1

--- a/solution.py
+++ b/solution.py
@@ -111,8 +111,10 @@
 
 
 def kernel(
+    c_in, x1_in, y1_in, x2_in, y2_in, sig_in, adj_in, ay_in, ax_in, pick_in, place_in,
+    out_any,
     c_ref, x1_ref, y1_ref, x2_ref, y2_ref, sig_ref, adj_ref, ay_ref, ax_ref, pick_ref, place_ref,
-    out_ref,
+    out_ref, load_sem,
     tiles, mask_x, mask_y, ext, send_first, send_last, recv_first, recv_last,
     rows_low, rows_high, recv_low, recv_high,
     mapped, mapped_y2, state, edge, state_z,
@@ -129,6 +131,18 @@
     for peer in (x_up, x_down, y_up, y_down, z_other):
         pl.semaphore_signal(barrier, inc=1, device_id=peer, device_id_type=MESH)
 
+    pairs = (
+        (sig_in, sig_ref), (x2_in, x2_ref), (y2_in, y2_ref), (c_in, c_ref), (x1_in, x1_ref),
+        (y1_in, y1_ref), (pick_in, pick_ref), (adj_in, adj_ref), (place_in, place_ref),
+        (ay_in, ay_ref), (ax_in, ax_ref),
+    )
+    loads = [
+        pltpu.make_async_copy(source, target, load_sem.at[i])
+        for i, (source, target) in enumerate(pairs)
+    ]
+    for load in loads:
+        load.start()
+
     def remote(index, source, target, peer):
         return pltpu.make_async_remote_copy(
             src_ref=source,
@@ -142,6 +156,8 @@
     lane = lax.broadcasted_iota(jnp.int32, (8, 128), 1)
     lane_wide = lax.broadcasted_iota(jnp.int32, (32, 128), 1)
 
+    for load in loads[:7]:
+        load.wait()
     lane_tile = lax.broadcasted_iota(jnp.int32, (4, 64), 1) // 16
     row_half = lax.broadcasted_iota(jnp.int32, (8, 64), 0) < 4
     for c in range(2):
@@ -205,6 +221,7 @@
     for copy in y_copies:
         copy.start()
 
+    loads[7].wait()
     adj_ext[...] = jnp.zeros_like(adj_ext)
     for i in range(20):
         adj_ext[i // 4, i % 4 + 1, 8:40] = adj_ref[i // 4, i % 4]
@@ -231,6 +248,8 @@
             target[v, 0, 8:40] = jnp.where(gz > 0, plane, 0.0)
             target[v, 5, 8:40] = jnp.where(gz > 0, 0.0, plane)
 
+    for load in loads[8:]:
+        load.wait()
     for copy in y_copies:
         copy.wait()
     joined = recv_first[...].astype(f32) + recv_last[...].astype(f32)
@@ -287,8 +306,8 @@
                 )
         mapped[:, at : at + 8] = total.reshape(40, 8, 256)
 
-    def synthesize(cv, carry):
-        for z in range(4):
+    def synthesize(order, cv, carry):
+        for z in order:
             p = cv * 4 + z
             exact = mapped[p]
             coarse_bits = exact.astype(bf16)
@@ -305,9 +324,15 @@
             edge[cv, z] = whole[8:40, 128:256] + extra[:, 128:256]
         return carry
 
-    lax.fori_loop(0, 10, synthesize, 0)
+    def synthesize_sides(pair, carry):
+        for j in range(5):
+            synthesize((z_side,), 5 * pair + j, carry)
+        return carry
+
+    lax.fori_loop(0, 2, synthesize_sides, 0)
     state_copy = remote(4, state.at[:, z_side + 1, 8:40], state_z, z_other)
     state_copy.start()
+    lax.fori_loop(0, 10, functools.partial(synthesize, (gz, gz + 1, gz + 2)), 0)
     state_copy.wait()
     for cv in range(10):
         plane = state_z[cv]
@@ -405,16 +430,32 @@
         copy.wait()
     fill_rims(mid_ext, mid_edge, 1)
     rate(5, mid_ext, mid_edge, finish_second)
+    store = pltpu.make_async_copy(out_ref, out_any, load_sem.at[11])
+    store.start()
+    store.wait()
 
 
 def shards(coarse, detail_x1, detail_y1, detail_x2, detail_y2, significance, adjoint):
-    vmem = pl.BlockSpec(memory_space=pltpu.VMEM)
+    anywhere = pl.BlockSpec(memory_space=pl.ANY)
     return pl.pallas_call(
         kernel,
         out_shape=jax.ShapeDtypeStruct(adjoint.shape, f32),
-        in_specs=[vmem] * 11,
-        out_specs=vmem,
+        in_specs=[pl.BlockSpec(memory_space=pltpu.HBM)] * 11,
+        out_specs=anywhere,
         scratch_shapes=[
+            pltpu.VMEM((320, 32), bf16),
+            pltpu.VMEM((320, 32), bf16),
+            pltpu.VMEM((640, 32), bf16),
+            pltpu.VMEM((640, 64), bf16),
+            pltpu.VMEM((1280, 64), bf16),
+            pltpu.VMEM((2, 4, 4, 4), jnp.int32),
+            pltpu.VMEM((5, 4, 32, 128), f32),
+            pltpu.VMEM((4, 128, 256), bf16),
+            pltpu.VMEM((48, 128), bf16),
+            pltpu.VMEM((2, 16, 64), bf16),
+            pltpu.VMEM((8, 128), f32),
+            pltpu.VMEM((5, 4, 32, 128), f32),
+            pltpu.SemaphoreType.DMA((12,)),
             pltpu.VMEM((2, 4, 8, 64), f32),
             pltpu.VMEM((2, 4, 16, 64), f32),
             pltpu.VMEM((2, 4, 32, 64), f32),
@@ -447,7 +488,7 @@
             pltpu.SemaphoreType.DMA((15,)),
             pltpu.SemaphoreType.DMA((15,)),
         ],
-        compiler_params=pltpu.CompilerParams(collective_id=0, has_side_effects=True),
+        compiler_params=pltpu.CompilerParams(collective_id=0, has_side_effects=True, vmem_limit_bytes=24*1024*1024),
     )(
         coarse.reshape(320, 32),
         detail_x1.reshape(320, 32),

time: 29.5 us -> 34.9 us (1.18)
  local copies, waits for them, and re-layouts: 1.72 us -> 9.35 us
  Pallas kernels: 27.6 us -> 25 us
    unnamed x1 -> x23, local copies, waits for them, and re-layouts: 1.72 us -> 9.35 us
    pallas_call x1, Pallas kernels: 27.6 us -> 25 us  [shards(): pl.pallas_call(kernel, out_shape=jax.ShapeDtypeStruct(adjoint.shape, f32)...]
where the time goes in v2:
time: 34.9 us; the launch traced here: 34.4 us
  Pallas kernels  25 us (72%)
  local copies, waits for them, and re-layouts  9.35 us (27%)
    pallas_call x1, Pallas kernels, shards(): pl.pallas_call(kernel, out_shape=jax.ShapeDtypeStruct(adjoint.shape, f32)...  25 us
    unnamed x23, local copies, waits for them, and re-layouts  9.35 us

profile of v2, /device:TPU:0, one launch (start us, length us, event | category | flops | bytes accessed | tf_op | source)
XLA Modules:
  0.0 34.4 jit_solution(11191259244671958195)
XLA Ops:
  0.0 0.0 copy-start.9
  0.0 0.0 copy-start.10
  0.0 0.7 %copy-done.9 = bf16[2,16,64]{2,1,0:T(8,128)(2,1)S(1)} copy-done((bf16[2,16,64]{2,1,0:T(8,128)(2,1)S(1)}, bf16[2,16,64]{2,1,0:T(8,128)(2,1)}, u32[]{:S(2)}) %copy-start.9) | copy-done | bytes 4120
  0.7 0.0 copy-done.10
  0.7 0.0 copy-start
  0.7 1.0 %copy-done = bf16[2,5,4,32,64]{4,3,2,1,0:T(8,128)(2,1)S(1)} copy-done((bf16[2,5,4,32,64]{4,3,2,1,0:T(8,128)(2,1)S(1)}, bf16[2,5,4,32,64]{4,3,2,1,0:T(8,128)(2,1)}, u32[]{:S(2)}) %copy-start) | copy-done | bytes 163864
  1.7 0.0 copy-start.1
  1.7 1.0 %copy-done.1 = f32[5,4,32,128]{3,2,1,0:T(8,128)S(1)} copy-done((f32[5,4,32,128]{3,2,1,0:T(8,128)S(1)}, f32[5,4,32,128]{3,2,1,0:T(8,128)}, u32[]{:S(2)}) %copy-start.1) | copy-done | bytes 327704
  2.6 0.0 copy-start.2
  2.7 0.9 %copy-done.2 = bf16[4,128,256]{2,1,0:T(8,128)(2,1)S(1)} copy-done((bf16[4,128,256]{2,1,0:T(8,128)(2,1)S(1)}, bf16[4,128,256]{2,1,0:T(8,128)(2,1)}, u32[]{:S(2)}) %copy-start.2) | copy-done | bytes 262168
  3.6 0.0 copy-start.3
  3.6 0.9 %copy-done.3 = bf16[2,5,4,16,32]{4,3,2,1,0:T(8,128)(2,1)S(1)} copy-done((bf16[2,5,4,16,32]{4,3,2,1,0:T(8,128)(2,1)S(1)}, bf16[2,5,4,16,32]{4,3,2,1,0:T(8,128)(2,1)}, u32[]{:S(2)}) %copy-start.3) | copy-done | bytes 40984
  4.5 0.0 copy-start.4
  4.5 0.9 %copy-done.4 = bf16[2,5,4,16,64]{4,3,2,1,0:T(8,128)(2,1)S(1)} copy-done((bf16[2,5,4,16,64]{4,3,2,1,0:T(8,128)(2,1)S(1)}, bf16[2,5,4,16,64]{4,3,2,1,0:T(8,128)(2,1)}, u32[]{:S(2)}) %copy-start.4) | copy-done | bytes 81944
  5.4 0.0 copy-start.5
  5.4 0.9 %copy-done.5 = bf16[2,5,4,8,32]{4,3,2,1,0:T(8,128)(2,1)S(1)} copy-done((bf16[2,5,4,8,32]{4,3,2,1,0:T(8,128)(2,1)S(1)}, bf16[2,5,4,8,32]{4,3,2,1,0:T(8,128)(2,1)}, u32[]{:S(2)}) %copy-start.5) | copy-done | bytes 20504
  6.3 0.0 copy-start.6
  6.3 0.9 %copy-done.6 = bf16[2,5,4,8,32]{4,3,2,1,0:T(8,128)(2,1)S(1)} copy-done((bf16[2,5,4,8,32]{4,3,2,1,0:T(8,128)(2,1)S(1)}, bf16[2,5,4,8,32]{4,3,2,1,0:T(8,128)(2,1)}, u32[]{:S(2)}) %copy-start.6) | copy-done | bytes 20504
  7.2 0.0 copy-start.7
  7.2 0.7 %copy-done.7 = s32[2,4,4,4]{3,2,1,0:T(4,128)S(1)} copy-done((s32[2,4,4,4]{3,2,1,0:T(4,128)S(1)}, s32[2,4,4,4]{3,2,1,0:T(4,128)}, u32[]{:S(2)}) %copy-start.7) | copy-done | bytes 536
  7.9 0.0 copy-start.8
  7.9 0.7 %copy-done.8 = bf16[48,128]{1,0:T(8,128)(2,1)S(1)} copy-done((bf16[48,128]{1,0:T(8,128)(2,1)S(1)}, bf16[48,128]{1,0:T(8,128)(2,1)}, u32[]{:S(2)}) %copy-start.8) | copy-done | bytes 12312
  8.6 25.0 %shard_map.109 = f32[5,4,32,128]{3,2,1,0:T(8,128)S(1)} custom-call(bf16[320,32]{1,0:T(8,128)(2,1)S(1)} %bitcast.8, bf16[320,32]{1,0:T(8,128)(2,1)S(1)} %bitcast.9, bf16[640,32]{1,0:T(8,128)(2,1)S(1)} %bitcast.6, bf16[640,64]{1,0:T(8,128)(2,1)S(1)} %bitcast.7, bf16[1280,64]{1,0:T(8,128)(2,1)S(1)} %bitcast.5, s32[2,4,4,4]{3,2,1,0:T(4,128)S(1)} %copy-done.7, ...), custom_call_target="tpu_custom_call" | custom-call | tf_op jit(solution)/shard_map/pallas_call | solution.py:440
  33.7 0.7 %copy.13 = f32[5,4,32,128]{3,2,1,0:T(8,128)} copy(f32[5,4,32,128]{3,2,1,0:T(8,128)S(1)} %shard_map.109) | data formatting | bytes 655360
Async XLA Ops:
  0.0 0.7 %copy-start.9 = (bf16[2,16,64]{2,1,0:T(8,128)(2,1)S(1)}, bf16[2,16,64]{2,1,0:T(8,128)(2,1)}, u32[]{:S(2)}) copy-start(bf16[2,16,64]{2,1,0:T(8,128)(2,1)} %constant.10.clone.pick_in) | copy-start | bytes 12292
  0.0 0.7 %copy-start.10 = (f32[8,128]{1,0:T(8,128)S(1)}, f32[8,128]{1,0:T(8,128)}, u32[]{:S(2)}) copy-start(f32[8,128]{1,0:T(8,128)} %constant.11.clone.place_in) | copy-start | bytes 12292
  0.7 1.0 %copy-start = (bf16[2,5,4,32,64]{4,3,2,1,0:T(8,128)(2,1)S(1)}, bf16[2,5,4,32,64]{4,3,2,1,0:T(8,128)(2,1)}, u32[]{:S(2)}) copy-start(bf16[2,5,4,32,64]{4,3,2,1,0:T(8,128)(2,1)} %param.15) | copy-start | bytes 491524
  1.7 1.0 %copy-start.1 = (f32[5,4,32,128]{3,2,1,0:T(8,128)S(1)}, f32[5,4,32,128]{3,2,1,0:T(8,128)}, u32[]{:S(2)}) copy-start(f32[5,4,32,128]{3,2,1,0:T(8,128)} %adj_in.1) | copy-start | bytes 983044
  2.6 0.9 %copy-start.2 = (bf16[4,128,256]{2,1,0:T(8,128)(2,1)S(1)}, bf16[4,128,256]{2,1,0:T(8,128)(2,1)}, u32[]{:S(2)}) copy-start(bf16[4,128,256]{2,1,0:T(8,128)(2,1)} %constant.8.clone.ay_in) | copy-start | bytes 786436
  3.6 0.9 %copy-start.3 = (bf16[2,5,4,16,32]{4,3,2,1,0:T(8,128)(2,1)S(1)}, bf16[2,5,4,16,32]{4,3,2,1,0:T(8,128)(2,1)}, u32[]{:S(2)}) copy-start(bf16[2,5,4,16,32]{4,3,2,1,0:T(8,128)(2,1)} %param.13) | copy-start | bytes 122884
  4.5 0.9 %copy-start.4 = (bf16[2,5,4,16,64]{4,3,2,1,0:T(8,128)(2,1)S(1)}, bf16[2,5,4,16,64]{4,3,2,1,0:T(8,128)(2,1)}, u32[]{:S(2)}) copy-start(bf16[2,5,4,16,64]{4,3,2,1,0:T(8,128)(2,1)} %param.14) | copy-start | bytes 245764
  5.4 0.9 %copy-start.5 = (bf16[2,5,4,8,32]{4,3,2,1,0:T(8,128)(2,1)S(1)}, bf16[2,5,4,8,32]{4,3,2,1,0:T(8,128)(2,1)}, u32[]{:S(2)}) copy-start(bf16[2,5,4,8,32]{4,3,2,1,0:T(8,128)(2,1)} %param.11) | copy-start | bytes 61444
  6.3 0.9 %copy-start.6 = (bf16[2,5,4,8,32]{4,3,2,1,0:T(8,128)(2,1)S(1)}, bf16[2,5,4,8,32]{4,3,2,1,0:T(8,128)(2,1)}, u32[]{:S(2)}) copy-start(bf16[2,5,4,8,32]{4,3,2,1,0:T(8,128)(2,1)} %param.12) | copy-start | bytes 61444
  7.2 0.7 %copy-start.7 = (s32[2,4,4,4]{3,2,1,0:T(4,128)S(1)}, s32[2,4,4,4]{3,2,1,0:T(4,128)}, u32[]{:S(2)}) copy-start(s32[2,4,4,4]{3,2,1,0:T(4,128)} %sig_in.1) | copy-start | bytes 1540
  7.9 0.7 %copy-start.8 = (bf16[48,128]{1,0:T(8,128)(2,1)S(1)}, bf16[48,128]{1,0:T(8,128)(2,1)}, u32[]{:S(2)}) copy-start(bf16[48,128]{1,0:T(8,128)(2,1)} %constant.9.clone.ax_in) | copy-start | bytes 36868

commit v3 on v2

--- a/solution.py
+++ b/solution.py
@@ -440,7 +440,7 @@
     return pl.pallas_call(
         kernel,
         out_shape=jax.ShapeDtypeStruct(adjoint.shape, f32),
-        in_specs=[pl.BlockSpec(memory_space=pltpu.HBM)] * 11,
+        in_specs=[anywhere] * 11,
         out_specs=anywhere,
         scratch_shapes=[
             pltpu.VMEM((320, 32), bf16),
@@ -488,7 +488,7 @@
             pltpu.SemaphoreType.DMA((15,)),
             pltpu.SemaphoreType.DMA((15,)),
         ],
-        compiler_params=pltpu.CompilerParams(collective_id=0, has_side_effects=True, vmem_limit_bytes=24*1024*1024),
+        compiler_params=pltpu.CompilerParams(collective_id=0, has_side_effects=True),
     )(
         coarse.reshape(320, 32),
         detail_x1.reshape(320, 32),

time: 34.9 us -> 27.6 us (0.79)
  local copies, waits for them, and re-layouts: 9.35 us -> 1.72 us
  Pallas kernels: 25 us -> 25.6 us
    unnamed x23 -> x1, local copies, waits for them, and re-layouts: 9.35 us -> 1.72 us
    pallas_call x1, Pallas kernels: 25 us -> 25.6 us  [shards(): pl.pallas_call(kernel, out_shape=jax.ShapeDtypeStruct(adjoint.shape, f32)...]
where the time goes in v3:
time: 27.6 us; the launch traced here: 27.4 us
  Pallas kernels  25.6 us (93%)
  local copies, waits for them, and re-layouts  1.72 us (6%)
    pallas_call x1, Pallas kernels, shards(): pl.pallas_call(kernel, out_shape=jax.ShapeDtypeStruct(adjoint.shape, f32)...  25.6 us
    unnamed x1, local copies, waits for them, and re-layouts  1.72 us

profile of v3, /device:TPU:0, one launch (start us, length us, event | category | flops | bytes accessed | tf_op | source)
XLA Modules:
  0.0 27.4 jit_solution(8818810561539951676)
XLA Ops:
  0.0 25.6 %shard_map.109 = f32[5,4,32,128]{3,2,1,0:T(8,128)} custom-call(bf16[320,32]{1,0:T(8,128)(2,1)} %bitcast.8, bf16[320,32]{1,0:T(8,128)(2,1)} %bitcast.9, bf16[640,32]{1,0:T(8,128)(2,1)} %bitcast.6, bf16[640,64]{1,0:T(8,128)(2,1)} %bitcast.7, bf16[1280,64]{1,0:T(8,128)(2,1)} %bitcast.5, s32[2,4,4,4]{3,2,1,0:T(4,128)} %sig_in.1, f32[5,4,32,128]{3,2,1,0:T(8,128)} %adj_in.1, ...), custom_call_target="tpu_custom_call" | custom-call | tf_op jit(solution)/shard_map/pallas_call | solution.py:440
  25.6 1.7 %copy.13 = f32[5,4,32,128]{3,2,1,0:T(8,128)} copy(f32[5,4,32,128]{3,2,1,0:T(8,128)} %shard_map.109) | data formatting | bytes 655360

commit v4 on v3

--- a/solution.py
+++ b/solution.py
@@ -119,7 +119,7 @@
     rows_low, rows_high, recv_low, recv_high,
     mapped, mapped_y2, state, edge, state_z,
     adj_ext, adj_edge, mid_ext, mid_edge,
-    ax_send, ax_recv, ay_send, ay_recv, az_send, az_recv, gx_terms, gz_terms,
+    ax_send, ax_recv, ay_send, ay_recv, az_recv, gx_terms, gy_terms, gz_terms,
     send_sem, recv_sem,
 ):
     gx, gy, gz = lax.axis_index("gx"), lax.axis_index("gy"), lax.axis_index("gz")
@@ -329,80 +329,91 @@
             synthesize((z_side,), 5 * pair + j, carry)
         return carry
 
-    lax.fori_loop(0, 2, synthesize_sides, 0)
-    state_copy = remote(4, state.at[:, z_side + 1, 8:40], state_z, z_other)
-    state_copy.start()
-    lax.fori_loop(0, 10, functools.partial(synthesize, (gz, gz + 1, gz + 2)), 0)
-    state_copy.wait()
-    for cv in range(10):
-        plane = state_z[cv]
-        state[cv, 0, 8:40] = jnp.where(gz > 0, plane, 0.0)
-        state[cv, 5, 8:40] = jnp.where(gz > 0, 0.0, plane)
-
     keep_bottom = jnp.where(gz > 0, 1.0, 0.0).astype(f32)
 
-    def rate(base, source, source_edge, finish):
-        def z_faces(k, carry):
-            for r in range(4):
-                at = slice(8 + 8 * r, 16 + 8 * r)
-                mean = [0.5 * (state[base + v, k, at] + state[base + v, k + 1, at]) for v in range(5)]
-                jump = [source[v, k + 1, at] - source[v, k, at] for v in range(5)]
-                terms = face(mean, jump, 2)
-                factor = jnp.where(k == 0, keep_bottom, 1.0)
-                for v in range(5):
-                    gz_terms[v, k, 8 * r : 8 * r + 8] = terms[v] * factor
+    def z_faces(base, source, k):
+        for r in range(4):
+            at = slice(8 + 8 * r, 16 + 8 * r)
+            mean = [0.5 * (state[base + v, k, at] + state[base + v, k + 1, at]) for v in range(5)]
+            jump = [source[v, k + 1, at] - source[v, k, at] for v in range(5)]
+            terms = face(mean, jump, 2)
+            for v in range(5):
+                gz_terms[v, k, 8 * r : 8 * r + 8] = terms[v]
+
+    def x_faces(base, source, z, r):
+        low_at, high_at = slice(7 + 8 * r, 15 + 8 * r), slice(8 + 8 * r, 16 + 8 * r)
+        mean = [
+            0.5 * (state[base + v, z + 1, low_at] + state[base + v, z + 1, high_at])
+            for v in range(5)
+        ]
+        jump = [source[v, z + 1, high_at] - source[v, z + 1, low_at] for v in range(5)]
+        terms = face(mean, jump, 0)
+        for v in range(5):
+            gx_terms[z, v, 8 * r : 8 * r + 8] = terms[v]
+
+    def inner_faces(base, source):
+        def middle_z(k, carry):
+            z_faces(base, source, k)
             return carry
 
-        lax.fori_loop(0, 5, z_faces, 0)
+        lax.fori_loop(1, 4, middle_z, 0)
 
         def plane(z, carry):
-            for r in range(5):
-                low_at, high_at = slice(7 + 8 * r, 15 + 8 * r), slice(8 + 8 * r, 16 + 8 * r)
-                mean = [
-                    0.5 * (state[base + v, z + 1, low_at] + state[base + v, z + 1, high_at])
-                    for v in range(5)
-                ]
-                jump = [source[v, z + 1, high_at] - source[v, z + 1, low_at] for v in range(5)]
-                terms = face(mean, jump, 0)
-                for v in range(5):
-                    gx_terms[v, 8 * r : 8 * r + 8] = terms[v]
+            for r in range(1, 4):
+                x_faces(base, source, z, r)
             for r in range(4):
                 at, rows = slice(8 + 8 * r, 16 + 8 * r), slice(8 * r, 8 * r + 8)
                 here = [state[base + v, z + 1, at] for v in range(5)]
+                adj = [source[v, z + 1, at] for v in range(5)]
+                terms = face(
+                    [0.5 * (a + pltpu.roll(a, 127, 1)) for a in here],
+                    [pltpu.roll(a, 127, 1) - a for a in adj],
+                    1,
+                )
+                for v in range(5):
+                    gy_terms[z, v, rows] = terms[v]
+            return carry
+
+        lax.fori_loop(0, 4, plane, 0)
+
+    def rate(base, source, source_edge, finish):
+        z_faces(base, source, 0)
+        gz_terms[:, 0] = gz_terms[:, 0] * keep_bottom
+        z_faces(base, source, 4)
+
+        def plane(z, carry):
+            x_faces(base, source, z, 0)
+            x_faces(base, source, z, 4)
+            for r in range(4):
+                at, rows = slice(8 + 8 * r, 16 + 8 * r), slice(8 * r, 8 * r + 8)
                 rim = [edge[base + v, z, rows] for v in range(5)]
                 adj = [source[v, z + 1, at] for v in range(5)]
                 adj_rim = [source_edge[v, z, rows] for v in range(5)]
 
-                def ahead(a, b):
-                    return pltpu.roll(jnp.where(lane == 0, b, a), 127, 1)
-
-                def behind(a, b):
-                    return pltpu.roll(jnp.where(lane == 127, b, a), 1, 1)
-
-                adj_up = [ahead(adj[v], adj_rim[v]) for v in range(5)]
-                adj_down = [behind(adj[v], adj_rim[v]) for v in range(5)]
-                up = face(
-                    [0.5 * (here[v] + ahead(here[v], rim[v])) for v in range(5)],
-                    [adj_up[v] - adj[v] for v in range(5)],
-                    1,
-                )
-                down = face(
-                    [0.5 * (here[v] + behind(here[v], rim[v])) for v in range(5)],
-                    [adj[v] - adj_down[v] for v in range(5)],
+                def across(a):
+                    return jnp.where(lane == 0, pltpu.roll(a, 1, 1), pltpu.roll(a, 127, 1))
+
+                jump = [adj_rim[v] - across(adj[v]) for v in range(5)]
+                terms = face(
+                    [0.5 * (rim[v] + across(state[base + v, z + 1, at])) for v in range(5)],
+                    [jnp.where(lane == 0, gap, -gap) for gap in jump],
                     1,
                 )
                 for v in range(5):
+                    held = gy_terms[z, v, rows]
+                    up = jnp.where(lane == 127, pltpu.roll(terms[v], 127, 1), held)
+                    down = pltpu.roll(jnp.where(lane == 127, terms[v], held), 1, 1)
                     halves = (
-                        up[v]
-                        + down[v]
-                        + gx_terms[v, rows]
-                        + gx_terms[v, 8 * r + 1 : 8 * r + 9]
+                        up
+                        + down
+                        + gx_terms[z, v, rows]
+                        + gx_terms[z, v, 8 * r + 1 : 8 * r + 9]
                         + gz_terms[v, z, rows]
                         + gz_terms[v, z + 1, rows]
                     )
                     around = (
-                        adj_up[v]
-                        + adj_down[v]
+                        pltpu.roll(jnp.where(lane == 0, adj_rim[v], adj[v]), 127, 1)
+                        + pltpu.roll(jnp.where(lane == 127, adj_rim[v], adj[v]), 1, 1)
                         + source[v, z + 1, 7 + 8 * r : 15 + 8 * r]
                         + source[v, z + 1, 9 + 8 * r : 17 + 8 * r]
                         + source[v, z, at]
@@ -413,6 +424,17 @@
 
         lax.fori_loop(0, 4, plane, 0)
 
+    lax.fori_loop(0, 2, synthesize_sides, 0)
+    state_copy = remote(4, state.at[:, z_side + 1, 8:40], state_z, z_other)
+    state_copy.start()
+    lax.fori_loop(0, 10, functools.partial(synthesize, (gz, gz + 1, gz + 2)), 0)
+    inner_faces(0, adj_ext)
+    state_copy.wait()
+    for cv in range(10):
+        plane = state_z[cv]
+        state[cv, 0, 8:40] = jnp.where(gz > 0, plane, 0.0)
+        state[cv, 5, 8:40] = jnp.where(gz > 0, 0.0, plane)
+
     def finish_first(v, z, rows, at, value):
         held = adj_ext[v, z + 1, at]
         mid_ext[v, z + 1, at] = held + time_step * value
@@ -422,10 +444,11 @@
         out_ref[v, z, rows] += 0.5 * time_step * value
 
     rate(0, adj_ext, adj_edge, finish_first)
+    mid_copies = rim_copies(mid_ext.at[:, z_side + 1, 8:40], 1)
     pack_rims(mid_ext, 1)
-    mid_copies = rim_copies(mid_ext.at[:, z_side + 1, 8:40], 1)
-    for copy in mid_copies:
+    for copy in mid_copies[2:4] + mid_copies[0:2] + mid_copies[4:5]:
         copy.start()
+    inner_faces(5, mid_ext)
     for copy in mid_copies:
         copy.wait()
     fill_rims(mid_ext, mid_edge, 1)
@@ -481,9 +504,9 @@
             pltpu.VMEM((2, 2, 24, 128), f32),
             pltpu.VMEM((2, 2, 32, 128), f32),
             pltpu.VMEM((2, 2, 32, 128), f32),
-            pltpu.VMEM((8, 128), f32),
             pltpu.VMEM((2, 5, 32, 128), f32),
-            pltpu.VMEM((5, 40, 128), f32),
+            pltpu.VMEM((4, 5, 40, 128), f32),
+            pltpu.VMEM((4, 5, 32, 128), f32),
             pltpu.VMEM((5, 5, 32, 128), f32),
             pltpu.SemaphoreType.DMA((15,)),
             pltpu.SemaphoreType.DMA((15,)),

time: 27.6 us -> 28.8 us (1.043)
  Pallas kernels: 25.6 us -> 26.8 us
    pallas_call x1, Pallas kernels: 25.6 us -> 26.8 us  [shards(): pl.pallas_call(kernel, out_shape=jax.ShapeDtypeStruct(adjoint.shape, f32)...]
where the time goes in v4:
time: 28.8 us; the launch traced here: 28.5 us
  Pallas kernels  26.8 us (93%)
  local copies, waits for them, and re-layouts  1.72 us (6%)
    pallas_call x1, Pallas kernels, shards(): pl.pallas_call(kernel, out_shape=jax.ShapeDtypeStruct(adjoint.shape, f32)...  26.8 us
    unnamed x1, local copies, waits for them, and re-layouts  1.72 us

profile of v4, /device:TPU:0, one launch (start us, length us, event | category | flops | bytes accessed | tf_op | source)
XLA Modules:
  0.0 28.5 jit_solution(11727459486480445829)
XLA Ops:
  0.0 26.8 %shard_map.109 = f32[5,4,32,128]{3,2,1,0:T(8,128)} custom-call(bf16[320,32]{1,0:T(8,128)(2,1)} %bitcast.8, bf16[320,32]{1,0:T(8,128)(2,1)} %bitcast.9, bf16[640,32]{1,0:T(8,128)(2,1)} %bitcast.6, bf16[640,64]{1,0:T(8,128)(2,1)} %bitcast.7, bf16[1280,64]{1,0:T(8,128)(2,1)} %bitcast.5, s32[2,4,4,4]{3,2,1,0:T(4,128)} %sig_in.1, f32[5,4,32,128]{3,2,1,0:T(8,128)} %adj_in.1, ...), custom_call_target="tpu_custom_call" | custom-call | tf_op jit(solution)/shard_map/pallas_call | solution.py:463
  26.8 1.7 %copy.13 = f32[5,4,32,128]{3,2,1,0:T(8,128)} copy(f32[5,4,32,128]{3,2,1,0:T(8,128)} %shard_map.109) | data formatting | bytes 655360

commit v5 on v3

--- a/solution.py
+++ b/solution.py
@@ -188,11 +188,13 @@
         send_first[:, begin:end] = ends[0:8].astype(bf16)
         send_last[:, begin:end] = ends[8:16].astype(bf16)
 
-    def pack_rims(source, which):
+    def pack_rows(source, which):
         for i in range(20):
             v, z = i // 4, i % 4
             ax_send[which, 0, i : i + 1] = source[v, z + 1, 8:9]
             ax_send[which, 1, i : i + 1] = source[v, z + 1, 39:40]
+
+    def pack_columns(source, which):
         first = jnp.zeros((32, 128), f32)
         last = jnp.zeros((32, 128), f32)
         for i in range(20):
@@ -225,7 +227,8 @@
     adj_ext[...] = jnp.zeros_like(adj_ext)
     for i in range(20):
         adj_ext[i // 4, i % 4 + 1, 8:40] = adj_ref[i // 4, i % 4]
-    pack_rims(adj_ext, 0)
+    pack_rows(adj_ext, 0)
+    pack_columns(adj_ext, 0)
     adj_copies = rim_copies(adj_ref.at[:, z_side], 0)
     for copy in adj_copies:
         copy.start()
@@ -235,14 +238,17 @@
         ext[begin:end, 0:width] = value.astype(f32)
     mid_ext[...] = jnp.zeros_like(mid_ext)
 
-    def fill_rims(target, target_edge, which):
+    def fill_columns(target_edge, which):
+        for i in range(20):
+            target_edge[i // 4, i % 4] = jnp.where(
+                lane_wide == 0, ay_recv[which, 1, :, i : i + 1], ay_recv[which, 0, :, i : i + 1]
+            )
+
+    def fill_rims(target, which):
         for i in range(20):
             v, z = i // 4, i % 4
             target[v, z + 1, 7:8] = ax_recv[which, 0, i : i + 1]
             target[v, z + 1, 40:41] = ax_recv[which, 1, i : i + 1]
-            target_edge[v, z] = jnp.where(
-                lane_wide == 0, ay_recv[which, 1, :, i : i + 1], ay_recv[which, 0, :, i : i + 1]
-            )
         for v in range(5):
             plane = az_recv[which, v]
             target[v, 0, 8:40] = jnp.where(gz > 0, plane, 0.0)
@@ -287,7 +293,8 @@
 
     for copy in adj_copies:
         copy.wait()
-    fill_rims(adj_ext, adj_edge, 0)
+    fill_rims(adj_ext, 0)
+    fill_columns(adj_edge, 0)
 
     row_kind = lax.broadcasted_iota(jnp.int32, (320, 128), 0) % 8
     for copy in x_copies:
@@ -341,7 +348,7 @@
 
     keep_bottom = jnp.where(gz > 0, 1.0, 0.0).astype(f32)
 
-    def rate(base, source, source_edge, finish):
+    def rate(base, source, source_edge, finish, stores=()):
         def z_faces(k, carry):
             for r in range(4):
                 at = slice(8 + 8 * r, 16 + 8 * r)
@@ -356,6 +363,12 @@
         lax.fori_loop(0, 5, z_faces, 0)
 
         def plane(z, carry):
+            if stores:
+
+                @pl.when(z > 0)
+                def _():
+                    store(z - 1).start()
+
             for r in range(5):
                 low_at, high_at = slice(7 + 8 * r, 15 + 8 * r), slice(8 + 8 * r, 16 + 8 * r)
                 mean = [
@@ -413,6 +426,9 @@
 
         lax.fori_loop(0, 4, plane, 0)
 
+    def store(z):
+        return pltpu.make_async_copy(out_ref.at[:, z], out_any.at[:, z], load_sem.at[11 + z])
+
     def finish_first(v, z, rows, at, value):
         held = adj_ext[v, z + 1, at]
         mid_ext[v, z + 1, at] = held + time_step * value
@@ -422,17 +438,23 @@
         out_ref[v, z, rows] += 0.5 * time_step * value
 
     rate(0, adj_ext, adj_edge, finish_first)
-    pack_rims(mid_ext, 1)
     mid_copies = rim_copies(mid_ext.at[:, z_side + 1, 8:40], 1)
-    for copy in mid_copies:
+    pack_columns(mid_ext, 1)
+    for copy in mid_copies[2:4]:
         copy.start()
-    for copy in mid_copies:
+    pack_rows(mid_ext, 1)
+    for copy in mid_copies[0:2] + mid_copies[4:5]:
+        copy.start()
+    for copy in mid_copies[0:2] + mid_copies[4:5]:
         copy.wait()
-    fill_rims(mid_ext, mid_edge, 1)
-    rate(5, mid_ext, mid_edge, finish_second)
-    store = pltpu.make_async_copy(out_ref, out_any, load_sem.at[11])
-    store.start()
-    store.wait()
+    fill_rims(mid_ext, 1)
+    for copy in mid_copies[2:4]:
+        copy.wait()
+    fill_columns(mid_edge, 1)
+    rate(5, mid_ext, mid_edge, finish_second, stores=(0, 1, 2, 3))
+    store(3).start()
+    for z in range(4):
+        store(z).wait()
 
 
 def shards(coarse, detail_x1, detail_y1, detail_x2, detail_y2, significance, adjoint):
@@ -455,7 +477,7 @@
             pltpu.VMEM((2, 16, 64), bf16),
             pltpu.VMEM((8, 128), f32),
             pltpu.VMEM((5, 4, 32, 128), f32),
-            pltpu.SemaphoreType.DMA((12,)),
+            pltpu.SemaphoreType.DMA((15,)),
             pltpu.VMEM((2, 4, 8, 64), f32),
             pltpu.VMEM((2, 4, 16, 64), f32),
             pltpu.VMEM((2, 4, 32, 64), f32),

time: 27.6 us -> 27.6 us (level)
  no operation moved by 1% of the time
where the time goes in v5:
time: 27.6 us; the launch traced here: 27.3 us
  Pallas kernels  25.6 us (93%)
  local copies, waits for them, and re-layouts  1.72 us (6%)
    pallas_call x1, Pallas kernels, shards(): pl.pallas_call(kernel, out_shape=jax.ShapeDtypeStruct(adjoint.shape, f32)...  25.6 us
    unnamed x1, local copies, waits for them, and re-layouts  1.72 us

profile of v5, /device:TPU:0, one launch (start us, length us, event | category | flops | bytes accessed | tf_op | source)
XLA Modules:
  0.0 27.3 jit_solution(1082536559305774316)
XLA Ops:
  0.0 25.6 %shard_map.109 = f32[5,4,32,128]{3,2,1,0:T(8,128)} custom-call(bf16[320,32]{1,0:T(8,128)(2,1)} %bitcast.8, bf16[320,32]{1,0:T(8,128)(2,1)} %bitcast.9, bf16[640,32]{1,0:T(8,128)(2,1)} %bitcast.6, bf16[640,64]{1,0:T(8,128)(2,1)} %bitcast.7, bf16[1280,64]{1,0:T(8,128)(2,1)} %bitcast.5, s32[2,4,4,4]{3,2,1,0:T(4,128)} %sig_in.1, f32[5,4,32,128]{3,2,1,0:T(8,128)} %adj_in.1, ...), custom_call_target="tpu_custom_call" | custom-call | tf_op jit(solution)/shard_map/pallas_call | solution.py:462
  25.6 1.7 %copy.13 = f32[5,4,32,128]{3,2,1,0:T(8,128)} copy(f32[5,4,32,128]{3,2,1,0:T(8,128)} %shard_map.109) | data formatting | bytes 655360
